TPU v7x, 32 devices: a whole 2x2x4 slice. The times are simulated.
32 devices in a mesh: replica: 4 (over z), shard: 8 (over y, x, core).
Axes of the slice: x: 2, y: 2, z: 4, core: 2. Of those that a mesh axis runs over, the one named last changes fastest.
Arguments:
- activations: bfloat16 [4, 2048, 4096], P('replica', 'shard'), may hold values from -6 to 6
- head_inputs: bfloat16 [4, 2048, 4096], P('replica', 'shard'), may hold values from -6 to 6
- out_cotangent: bfloat16 [4, 2048, 4096], P('replica', 'shard'), may hold values from -6 to 6
- episode_spans: int32 [4, 4], P('replica'), may hold values from 1 to 8, 16 in all within a row
- last_valid: int32 [4, 4], P('replica'), may hold values from 1 to 128, as said below
- mixer_weight: bfloat16 [4096, 256], P('shard'), may hold values from -0.09375 to 0.09375
- step_weight: bfloat16 [4096, 64], P('shard'), may hold values from -0.09375 to 0.09375
- decay_log: float32 [64], replicated, may hold values from 0 to 2.77
- step_bias: float32 [64], replicated, may hold values from -6.9 to -2.3
- skip_gain: float32 [64], replicated, may hold values from -3 to 3
Outputs:
- inputs_grad: bfloat16 [4, 2048, 4096], P('replica', 'shard')
- activations_grad: bfloat16 [4, 2048, 4096], P('replica', 'shard')
- mixer_grad: float32 [4096, 256], P('shard')
- step_grad: float32 [4096, 64], P('shard')
- decay_grad: float32 [64], replicated
- bias_grad: float32 [64], replicated
- skip_grad: float32 [64], replicated
Inputs may be any that keep to these rules, and one draw needn't show every extreme that they name: `episode_spans`: each group's 4 episode lengths, in spans of 128 tokens, add up to 16. `last_valid`: tokens after the valid ones in an episode's last span are padding.
All inputs are finite; a program needn't handle non-finite values.
Results may differ from a plain program's by a relative error of at most 0.018.
Values may be sent and summed in bfloat16 or wider, within the bound.
A program may use at most 320 MiB of HBM per device.

v0:
```python
import jax
import jax.numpy as jnp
from jax import lax
from jax.sharding import PartitionSpec as P

STATE = 128
SPAN = 128


def entering_2(value, axis, combine, identity, reverse):
    count, index = (lax.axis_size(axis), lax.axis_index(axis))
    everything = jax.tree.map(
        lambda part, kind: lax.all_gather(part.astype(kind), axis),
        value,
        jax.tree.map(lambda a: jnp.bfloat16 if a.dtype == jnp.float32 else a.dtype, value),
    )
    start = jax.tree.map(
        lambda part, zero: jnp.broadcast_to(jnp.asarray(zero, part.dtype), part.shape),
        value,
        identity,
    )

    def step(k, before):
        at = count - 1 - k if reverse else k
        reached = at > index if reverse else at < index
        new = combine(
            before, jax.tree.map(lambda part, own: part[at].astype(own.dtype), everything, value)
        )
        return jax.tree.map(lambda a, b: jnp.where(reached, a, b), new, before)

    return lax.fori_loop(0, count, step, start)


def span_layout(episode_spans, last_valid, first_span, span_count):
    span_ids = first_span + jnp.arange(span_count, dtype=jnp.int32)
    starts = jnp.cumsum(episode_spans) - episode_spans
    finals = starts + episode_spans - 1
    resets = jnp.any(span_ids[:, None] == starts[None, :], axis=1)
    final_hit = span_ids[:, None] == finals[None, :]
    valid_count = jnp.sum(jnp.where(final_hit, last_valid[None, :] - SPAN, 0), axis=1) + SPAN
    offsets = jnp.arange(SPAN, dtype=jnp.int32)
    valid_mask = jnp.where(offsets[None, :] < valid_count[:, None], 1.0, 0.0).astype(jnp.float32)
    keep_flag = jnp.where(resets, 0.0, 1.0).astype(jnp.float32)
    return (valid_mask, keep_flag)


def span_end(mixers, step_sizes, inputs, decay_log):
    length = inputs.shape[0]
    head_count = decay_log.shape[0]
    per_head = inputs.reshape(length, head_count, -1)
    cumulative = jnp.cumsum(step_sizes * (-jnp.exp(decay_log))[None, :], axis=0)
    weights = jnp.exp(cumulative[-1][None, :] - cumulative) * step_sizes
    weighted = (per_head * weights[:, :, None]).astype(jnp.bfloat16)
    end_state = jnp.einsum(
        "lhp,ln->hpn", weighted, mixers[:, :STATE], preferred_element_type=jnp.float32
    )
    return (jnp.exp(cumulative[-1]), end_state)


def span_out(mixers, step_sizes, inputs, entering, decay_log, skip_gain, valid_mask):
    length = inputs.shape[0]
    head_count = decay_log.shape[0]
    per_head = inputs.reshape(length, head_count, -1)
    input_map = mixers[:, :STATE]
    output_map = mixers[:, STATE:]
    cumulative = jnp.cumsum(step_sizes * (-jnp.exp(decay_log))[None, :], axis=0)
    scores = lax.dot_general(
        output_map, input_map, (((1,), (1,)), ((), ())), preferred_element_type=jnp.float32
    )
    by_head = cumulative.T
    causal = jnp.arange(length)[:, None] >= jnp.arange(length)[None, :]
    gaps = jnp.where(causal[None], by_head[:, :, None] - by_head[:, None, :], -jnp.inf)
    mixing = jnp.exp(gaps) * scores[None] * step_sizes.T[:, None, :]
    mixing = mixing.astype(jnp.bfloat16)
    inner = jnp.einsum("hls,shp->lhp", mixing, per_head, preferred_element_type=jnp.float32)
    entering_low = entering.astype(jnp.bfloat16)
    carried = jnp.einsum(
        "ln,hpn->lhp", output_map, entering_low, preferred_element_type=jnp.float32
    )
    carried = carried * jnp.exp(cumulative)[:, :, None]
    total = inner + carried + skip_gain[None, :, None] * per_head
    return total.reshape(length, -1) * valid_mask[:, None]


def chain_step(earlier, later):
    return (earlier[0] * later[0], later[1] + later[0][:, None, None] * earlier[1])


def shards(
    activations,
    head_inputs,
    out_cotangent,
    episode_spans,
    last_valid,
    mixer_weight,
    step_weight,
    decay_log,
    step_bias,
    skip_gain,
):
    token_rows = activations[0]
    inputs_here = head_inputs[0]
    tokens_here = token_rows.shape[0]
    span_count = tokens_here // SPAN
    head_count = decay_log.shape[0]
    first_span = lax.axis_index("shard") * span_count
    valid_mask, keep_flag = span_layout(episode_spans[0], last_valid[0], first_span, span_count)
    flat_mask = valid_mask.reshape(-1)
    joined = jnp.concatenate([mixer_weight, step_weight], axis=1)
    gathered = lax.all_gather(joined, "shard", axis=0, tiled=True)
    projected = jnp.dot(token_rows, gathered, preferred_element_type=jnp.float32)
    mixers = projected[:, : 2 * STATE].astype(jnp.bfloat16)
    raw_steps = projected[:, 2 * STATE :] + step_bias[None, :]

    def end_part(mixers, raw_steps, inputs, decay_log):
        step_sizes = jax.nn.softplus(raw_steps) * flat_mask[:, None]
        return lax.map(
            lambda pieces: span_end(pieces[0], pieces[1], pieces[2], decay_log),
            (
                mixers.reshape(span_count, SPAN, -1),
                step_sizes.reshape(span_count, SPAN, -1),
                inputs.reshape(span_count, SPAN, -1),
            ),
        )

    def out_part(mixers, raw_steps, inputs, entering, decay_log, skip_gain):
        step_sizes = jax.nn.softplus(raw_steps) * flat_mask[:, None]
        return lax.map(
            lambda pieces: span_out(
                pieces[0], pieces[1], pieces[2], pieces[3], decay_log, skip_gain, pieces[4]
            ),
            (
                mixers.reshape(span_count, SPAN, -1),
                step_sizes.reshape(span_count, SPAN, -1),
                inputs.reshape(span_count, SPAN, -1),
                entering,
                valid_mask,
            ),
        )

    (decays, states), end_pull = jax.vjp(end_part, mixers, raw_steps, inputs_here, decay_log)
    factors = decays * keep_flag[:, None]
    identity_pair = (jnp.ones((head_count,), jnp.float32), jnp.zeros(states.shape[1:], jnp.float32))

    def fold_spans(running, pieces):
        return (chain_step(running, pieces), None)

    local_total, _ = lax.scan(fold_spans, identity_pair, (factors, states))
    before_dev = entering_2(local_total, "shard", chain_step, identity_pair, False)

    def pass_forward(carry, pieces):
        entering = carry * pieces[2]
        return (pieces[0][:, None, None] * carry + pieces[1], entering)

    _, entering = lax.scan(pass_forward, before_dev[1], (factors, states, keep_flag))
    _, out_pull = jax.vjp(out_part, mixers, raw_steps, inputs_here, entering, decay_log, skip_gain)
    cotangent = out_cotangent[0].astype(jnp.float32).reshape(span_count, SPAN, -1)
    mixer_first, raw_first, input_first, enter_grad, decay_first, skip_local = out_pull(cotangent)
    local_terms = enter_grad * keep_flag[:, None, None, None]
    back_total, _ = lax.scan(fold_spans, identity_pair, (factors, local_terms), reverse=True)
    after_dev = entering_2(back_total, "shard", chain_step, identity_pair, True)

    def pass_back(carry, pieces):
        return (pieces[0][:, None, None] * carry + pieces[1], carry)

    _, ends_grad = lax.scan(pass_back, after_dev[1], (factors, local_terms), reverse=True)
    decay_cot = jnp.sum(ends_grad * entering, axis=(2, 3))
    mixer_second, raw_second, input_second, decay_second = end_pull((decay_cot, ends_grad))
    mixer_cot = mixer_first + mixer_second
    raw_cot = raw_first + raw_second
    input_grad = input_first + input_second
    joined_cot = jnp.concatenate([mixer_cot, raw_cot.astype(jnp.bfloat16)], axis=1)
    back_rows = lax.dot_general(
        joined_cot, gathered, (((1,), (1,)), ((), ())), preferred_element_type=jnp.float32
    )
    grads_local = lax.dot_general(
        token_rows, joined_cot, (((0,), (0,)), ((), ())), preferred_element_type=jnp.float32
    )
    shared = lax.psum_scatter(
        grads_local.astype(jnp.bfloat16), "shard", scatter_dimension=0, tiled=True
    )
    summed = lax.psum(shared, "replica").astype(jnp.float32)
    small = lax.psum(
        (decay_first + decay_second, jnp.sum(raw_cot, axis=0), skip_local), ("replica", "shard")
    )
    return (
        input_grad[None],
        back_rows.astype(jnp.bfloat16)[None],
        summed[:, : 2 * STATE],
        summed[:, 2 * STATE :],
        small[0],
        small[1],
        small[2],
    )


def solution(mesh):
    return jax.shard_map(
        shards,
        mesh=mesh,
        in_specs=(
            P("replica", "shard", None),
            P("replica", "shard", None),
            P("replica", "shard", None),
            P("replica", None),
            P("replica", None),
            P("shard", None),
            P("shard", None),
            P(),
            P(),
            P(),
        ),
        out_specs=(
            P("replica", "shard", None),
            P("replica", "shard", None),
            P("shard", None),
            P("shard", None),
            P(),
            P(),
            P(),
        ),
        check_vma=False,
    )
```

profile of v0, /device:TPU:0, one launch (start us, length us, event | category | flops | bytes accessed | tf_op | source)
XLA Modules:
  0.0 563.7 jit_solution(1563798351276136029)
XLA Ops:
  11.0 4.1 copy.125
  16.2 29.2 %all-gather.8.cloned.1.call-done = bf16[4096,320]{1,0:T(8,128)(2,1)} async-done(((bf16[512,320]{1,0:T(8,128)(2,1)}), bf16[4096,320]{1,0:T(8,128)(2,1)}) %all-gather.8.cloned.1.call-update) | async-done | bytes 2621456 | tf_op jit(solution)/shard_map/all_gather | solution.py:110
  56.4 21.2 %while.194 = (s32[]{:T(128)}, f32[2,64]{1,0:T(2,128)S(1)}, f32[2,64,64,128]{3,2,1,0:T(8,128)}, f32[2,128,64]{2,1,0:T(8,128)S(1)}, f32[2,128,64,1]{1,2,3,0:T(8,12...) while((s32[]{:T(128)}, f32[2,64]{1,0:T(2,128)S(1)}, ...), condition=%wide.region_4.6_spmd, body=%wide.region_2.5_spmd.sunk | while | flops 137928704 | bytes 40800012 | solution.py:117
  78.3 7.0 %while.198 = (s32[]{:T(128)}, f32[64]{0:T(128)S(1)}, f32[64,64,128]{2,1,0:T(8,128)}, f32[2,64]{1,0:T(2,128)S(1)}, f32[2,64,64,128]{3,2,1,0:T(8,128)}, /*index=5*/s32[]{:T(128)}, s32[]{:T(128)}) while((s32[]{:T(128)}, f32[64]{0:T(128)S(1)}, f32[64,64,128]{2,1,0:T(8,128)}, f32[2,64]{1,0:T(2,128)S(1)}, f32[2,64,64,128]{3,2,1,0:T(8,128)}, ...), condition=%wide.region_7.9_spmd.clone, body=%wide.region_6.8_spmd.clone.sunk | while | flops 1572995 | bytes 6292832 | solution.py:148
  81.5 3.8 bitcast_add_fusion.13
  88.3 4.1 convert.12
  93.8 14.1 %all-reduce.5 = bf16[512]{0:T(512)(128)(2,1)S(1)} all-reduce(bf16[512]{0:T(512)(128)(2,1)S(1)} %dynamic-update-slice), channel_id=3, replica_groups=mesh['replica'=4,'shard'=8] {'shard'}, use_global_device_ids=true, to_apply=%add.5 | all-reduce | flops 512 | bytes 2048
  108.0 34.7 %all-gather.10.cloned.1.call-done = bf16[512,64,128]{2,1,0:T(8,128)(2,1)} async-done(((bf16[64,64,128]{2,1,0:T(8,128)(2,1)}), bf16[512,64,128]{2,1,0:T(8,128)(2,1)}) %all-gather.10.cloned.1.call-update) | async-done | bytes 8388624 | tf_op jit(solution)/shard_map/all_gather | solution.py:13
  142.7 27.9 %while.199 = (s32[]{:T(128)}, f32[64,64,128]{2,1,0:T(8,128)}, s32[]{:T(128)}, bf16[8,64,64,128]{3,2,1,0:T(8,128)(2,1)}, bf16[8,64]{1,0:T(8,128)(2,1)S(1)}, /*index=5*/s32[]{:T(128)}, s32[]{:T(128)}) while((s32[]{:T(128)}, f32[64,64,128]{2,1,0:T(8,128)}, s32[]{:T(128)}, bf16[8,64,64,128]{3,2,1,0:T(8,128)(2,1)}, ...), condition=%wide.region_9.11_spmd.clone, body=%wide.region_8.10_spmd.clone.sunk | while | flops 2621508 | bytes 5243625 | solution.py:31
  145.6 3.6 fusion.199
  149.2 3.6 fusion.199
  152.8 3.6 fusion.199
  156.3 3.6 fusion.199
  159.9 3.6 fusion.199
  163.5 3.6 fusion.199
  167.0 3.6 fusion.199
  173.1 15.8 %while.195 = (s32[]{:T(128)}, f32[64,64,128]{2,1,0:T(8,128)}, f32[2,64,64,128]{3,2,1,0:T(8,128)}, f32[2,64]{1,0:T(2,128)S(1)}, f32[2,64,64,128]{3,2,1,0:T(8,128)}, /*index=5*/f32[2]{0:T(128)S(1)}, s32[]{:T(128)}) while((s32[]{:T(128)}, f32[64,64,128]{2,1,0:T(8,128)}, f32[2,64,64,128]{3,2,1,0:T(8,128)}, f32[2,64]{1,0:T(2,128)S(1)}, ...), condition=%wide.region_11.13_spmd, body=%wide.region_10.12_spmd.sunk | while | flops 1572866 | bytes 27264892 | solution.py:155
  173.6 4.1 bitcast_dynamic-update-slice_fusion.23
  181.6 4.0 bitcast_dynamic-update-slice_fusion.23
  188.8 4.0 convert.56
  200.9 40.2 %while.197 = (s32[]{:T(128)}, bf16[2,128,128]{2,1,0:T(8,128)(2,1)}, bf16[2,128,128]{2,1,0:T(8,128)(2,1)S(1)}, f32[2,64,128,128]{3,2,1,0:T(8,128)}, f32[2,1,128,1...) while((s32[]{:T(128)}, bf16[2,128,128]{2,1,0:T(8,128)(2,1)}, ...), condition=%wide.region_14.16_spmd.clone, body=%wide.region_12.15_spmd.clone.sunk | while | flops 148373504 | bytes 75078808 | solution.py:128
  202.6 3.9 fusion.195
  222.7 3.9 fusion.195
  246.6 60.3 %while.200 = (s32[]{:T(128)}, f32[64]{0:T(128)}, f32[64]{0:T(128)}, bf16[2,128,256]{2,1,0:T(8,128)(2,1)}, f32[2,128,64]{2,1,0:T(8,128)}, /*index=5*/bf16[2,128,4...) while((s32[]{:T(128)}, f32[64]{0:T(128)}, f32[64]{0:T(128)}, ...), condition=%wide.region_24.26_spmd.clone, body=%wide.region_15.25_spmd.clone.sunk | while | flops 567435520 | bytes 130551072 | solution.py:128
  262.2 5.0 fusion.212
  292.3 5.0 fusion.212
  307.0 5.0 broadcast_multiply_fusion
  312.0 7.0 %while.201 = (s32[]{:T(128)}, f32[64]{0:T(128)S(1)}, f32[64,64,128]{2,1,0:T(8,128)}, f32[2,64]{1,0:T(2,128)S(1)}, f32[2,64,64,128]{3,2,1,0:T(8,128)}, /*index=5*/s32[]{:T(128)}, s32[]{:T(128)}) while((s32[]{:T(128)}, f32[64]{0:T(128)S(1)}, f32[64,64,128]{2,1,0:T(8,128)}, f32[2,64]{1,0:T(2,128)S(1)}, ...), condition=%wide.region_26.28_spmd.clone, body=%wide.region_25.27_spmd.clone.sunk | while | flops 1572996 | bytes 6292844 | solution.py:160
  315.2 3.8 bitcast_add_fusion.15
  322.1 13.2 %all-reduce.6 = bf16[512]{0:T(512)(128)(2,1)S(1)} all-reduce(bf16[512]{0:T(512)(128)(2,1)S(1)} %dynamic-update-slice.1), channel_id=5, replica_groups=mesh['replica'=4,'shard'=8] {'shard'}, use_global_device_ids=true, to_apply=%add.6 | all-reduce | flops 512 | bytes 2048
  335.5 40.8 %all-gather.12.cloned.1.call-done = bf16[512,64,128]{2,1,0:T(8,128)(2,1)} async-done(((bf16[64,64,128]{2,1,0:T(8,128)(2,1)}), bf16[512,64,128]{2,1,0:T(8,128)(2,1)}) %all-gather.12.cloned.1.call-update) | async-done | bytes 8388624 | tf_op jit(solution)/shard_map/all_gather | solution.py:13
  376.2 27.9 %while.202 = (s32[]{:T(128)}, f32[64,64,128]{2,1,0:T(8,128)}, s32[]{:T(128)}, bf16[8,64,64,128]{3,2,1,0:T(8,128)(2,1)}, bf16[8,64]{1,0:T(8,128)(2,1)S(1)}, /*index=5*/s32[]{:T(128)}, s32[]{:T(128)}, s32[]{:T(128)}, s32[]{:T(128)}) while((s32[]{:T(128)}, f32[64,64,128]{2,1,0:T(8,128)}, s32[]{:T(128)}, ...), condition=%wide.region_28.30_spmd.clone, body=%wide.region_27.29_spmd.clone.sunk | while | flops 2621512 | bytes 5243687 | solution.py:31
  379.2 3.6 fusion.219
  382.8 3.6 fusion.219
  386.3 3.6 fusion.219
  389.9 3.6 fusion.219
  393.5 3.6 fusion.219
  397.0 3.6 fusion.219
  400.6 3.6 fusion.219
  406.6 13.1 %while.196 = (s32[]{:T(128)}, f32[64,64,128]{2,1,0:T(8,128)}, f32[2,64,64,128]{3,2,1,0:T(8,128)}, f32[2,64]{1,0:T(2,128)S(1)}, f32[2,64,64,128]{3,2,1,0:T(8,128)}, /*index=5*/s32[]{:T(128)}) while((s32[]{:T(128)}, f32[64,64,128]{2,1,0:T(8,128)}, f32[2,64,64,128]{3,2,1,0:T(8,128)}, f32[2,64]{1,0:T(2,128)S(1)}, ...), condition=%wide.region_30.32_spmd, body=%wide.region_29.31_spmd.sunk | while | flops 1048579 | bytes 27263864 | solution.py:166
  413.2 3.3 bitcast_dynamic-update-slice_fusion.24
  419.7 7.0 %fusion.139 = (bf16[2,64,64,128]{3,2,1,0:T(8,128)(2,1)}, f32[2,64]{1,0:T(2,128)S(1)}) fusion(f32[2,64,64,128]{3,2,1,0:T(8,128)} %get-tuple-element.2433, f32[2,64,64,128]{3,2,1,0:T(8,128)} %get-tuple-element.2378), kind=kLoop, calls=%fused_computation.230 | loop fusion | flops 3145600 | bytes 10486272
  429.7 22.4 %while.203 = (s32[]{:T(128)}, f32[64]{0:T(128)S(1)}, bf16[2,128,256]{2,1,0:T(8,128)(2,1)}, f32[2,128,64]{2,1,0:T(8,128)}, bf16[2,128,4096]{1,2,0:T(8,128)(2,1)},...) while((s32[]{:T(128)}, f32[64]{0:T(128)S(1)}, ...), condition=%wide.region_37.39_spmd.clone, body=%wide.region_32.38_spmd.clone.sunk | while | flops 272179392 | bytes 18716728 | solution.py:117
  457.8 43.6 %reduce-scatter.2.cloned.1.call-done = bf16[512,320]{0,1:T(8,128)(2,1)} async-done(((bf16[4096,320]{0,1:T(8,128)(2,1)}), bf16[512,320]{0,1:T(8,128)(2,1)}) %reduce-scatter.2.cloned.1.call-update) | async-done | bytes 327696 | tf_op jit(solution)/shard_map/reduce_scatter | solution.py:179
  501.5 4.1 add.261
  505.5 4.1 copy.133
  509.7 39.5 %all-reduce.7 = (f32[64]{0:T(128)}, f32[64]{0:T(128)}, f32[64]{0:T(128)}) all-reduce(f32[64]{0:T(128)S(1)} %add.266, f32[64]{0:T(128)S(1)} %get-tuple-element.2556, f32[64]{0:T(128)S(1)} %copy-done.40), channel_id=1, replica_groups=mesh['replica'=4,'shard'=8] {'replica','shard'}, use_global_device_ids=true, to_apply=%region_40.42 | all-reduce | flops 192 | bytes 1536 | tf_op jit(solution)/shard_map/psum | solution.py:183
  549.1 4.5 fusion.120
  (438 shorter events, 209.3 us)
Async XLA Ops:
  7.2 38.2 %copy-start = (bf16[1,256,4096]{2,1,0:T(8,128)(2,1)S(1)}, bf16[1,256,4096]{2,1,0:T(8,128)(2,1)}, u32[]{:S(2)}) copy-start(bf16[1,256,4096]{2,1,0:T(8,128)(2,1)} %param.31) | copy-start | bytes 6291460
  7.2 38.2 %all-gather.8.cloned.1.call-start = ((), (), s32[]{:S(2)}) async-start(), calls=%async_computation.1 | async-start | bytes 3538944 | tf_op jit(solution)/shard_map/all_gather | solution.py:110
  10.1 132.6 %all-gather.10.cloned.1.call-start = ((), (), s32[]{:S(2)}) async-start(), calls=%async_computation.4 | async-start | bytes 9437184 | tf_op jit(solution)/shard_map/all_gather | solution.py:13
  11.0 4.1 copy-start.48
  11.0 4.3 copy-start.49
  11.0 4.5 copy-start.50
  16.2 32.1 %copy-start.43 = (f32[256]{0:T(256)}, f32[256]{0:T(256)S(1)}, u32[]{:S(2)}) copy-start(f32[256]{0:T(256)S(1)} %get-tuple-element.2579) | copy-start | bytes 3076
  16.2 32.8 %copy-start.45 = (f32[64]{0:T(128)S(1)}, f32[64]{0:T(128)}, u32[]{:S(2)}) copy-start(f32[64]{0:T(128)} %param.39) | copy-start | bytes 772
  58.8 3.1 copy-start.17
  69.3 3.1 copy-start.17
  88.1 288.2 %all-gather.12.cloned.1.call-start = ((), (), s32[]{:S(2)}) async-start(), calls=%async_computation.5 | async-start | bytes 9437184 | tf_op jit(solution)/shard_map/all_gather | solution.py:13
  88.3 4.1 copy-start.51
  173.6 4.1 copy-start.4
  181.6 4.0 copy-start.4
  188.8 4.0 copy-start.32
  188.8 4.0 copy-start.44
  213.9 4.0 copy-start.46
  215.4 3.1 copy-start.6
  234.0 4.0 copy-start.46
  235.4 3.1 copy-start.6
  247.3 10.6 %copy-start.27 = (f32[128]{0:T(128)}, f32[128]{0:T(128)S(1)}, u32[]{:S(2)}) copy-start(f32[128]{0:T(128)S(1)} %fusion.210) | copy-start | bytes 1540 | tf_op jit(solution)/shard_map/transpose(jvp())/while
  254.1 3.8 copy-start.9
  262.2 5.1 copy-start.7
  262.2 5.9 %copy-start.8 = (f32[2,128,64,64]{1,3,2,0:T(8,128)S(1)}, f32[2,128,64,64]{1,3,2,0:T(8,128)}, u32[]{:S(2)}) copy-start(f32[2,128,64,64]{1,3,2,0:T(8,128)} %get-tuple-element.3553) | copy-start | bytes 12582916 | tf_op jit(solution)/shard_map/transpose(jvp())/while
  271.4 4.2 copy-start.22
  271.4 4.9 copy-start.29
  271.4 4.9 copy-start.30
  271.4 4.9 copy-start.35
  271.4 4.9 copy-start.38
  277.4 10.5 %copy-start.27 = (f32[128]{0:T(128)}, f32[128]{0:T(128)S(1)}, u32[]{:S(2)}) copy-start(f32[128]{0:T(128)S(1)} %fusion.210) | copy-start | bytes 1540 | tf_op jit(solution)/shard_map/transpose(jvp())/while
  284.2 3.7 copy-start.9
  292.3 5.1 copy-start.7
  292.3 5.9 %copy-start.8 = (f32[2,128,64,64]{1,3,2,0:T(8,128)S(1)}, f32[2,128,64,64]{1,3,2,0:T(8,128)}, u32[]{:S(2)}) copy-start(f32[2,128,64,64]{1,3,2,0:T(8,128)} %get-tuple-element.3553) | copy-start | bytes 12582916 | tf_op jit(solution)/shard_map/transpose(jvp())/while
  301.5 4.2 copy-start.22
  301.5 4.9 copy-start.29
  301.5 4.9 copy-start.30
  301.5 4.9 copy-start.35
  301.5 4.9 copy-start.38
  306.9 5.0 copy-start.33
  306.9 5.0 copy-start.34
  321.8 179.6 %reduce-scatter.2.cloned.1.call-start = ((), (), s32[]{:S(2)}) async-start(), calls=%async_computation.2 | async-start | bytes 2949120 | tf_op jit(solution)/shard_map/reduce_scatter | solution.py:179
  406.6 3.3 copy-start.3
  413.2 3.3 copy-start.3
  436.5 3.7 copy-start.24
  447.8 3.7 copy-start.24
  457.8 95.8 %all-reduce.10.cloned.1.call-start = ((), (), s32[]{:S(2)}) async-start(), calls=%async_computation.3 | async-start | bytes 655360 | tf_op jit(solution)/shard_map/psum | solution.py:182
  505.5 4.1 copy-start.37
  505.5 4.1 copy-start.40
  (40 other events, 64.8 us)
Sparse Core Ops, SparseCore 0:
  10.4 34.8 all-gather.7
  88.2 54.4 all-gather.9
  321.9 54.2 all-gather.11
  457.9 43.4 reduce-scatter.1
  503.6 36.6 all-reduce.9
where the time goes:
time: 566 us; the launch traced here: 564 us
  other arithmetic  171 us (30%)
  waiting for transfers between devices  148 us (26%)
  local copies, waits for them, and re-layouts  112 us (20%)
  blocking collectives  66.8 us (12%)
  matrix products  48.8 us (9%)
  between operations  14.8 us (3%)
    all_gather x2, waiting for transfers between devices, entering_2(): lax.all_gather(part.astype(kind), axis)  75.5 us
    select_n x16, other arithmetic, step(): return jax.tree.map(lambda a, b: jnp.where(reached, a, b), new, before)  55.7 us
    reduce_scatter x1, waiting for transfers between devices, shards(): lax.psum_scatter(grads_local.astype(jnp.bfloat16), 'shard', scatter_dimen...  43.6 us
    psum x1, blocking collectives, shards(): lax.psum((decay_first + decay_second, jnp.sum(raw_cot, axis=0), skip_loca...  39.5 us
    all_gather x1, waiting for transfers between devices, shards(): gathered = lax.all_gather(joined, 'shard', axis=0, tiled=True)  29.2 us
    another operation x21, local copies, waits for them, and re-layouts  28.4 us
    unnamed x2, blocking collectives  27.3 us
    while x124, local copies, waits for them, and re-layouts  19.8 us
  transfers between devices with their start and end apart: 5, of which 4 were waited for; matrix products, arithmetic and copies ran while one was open for 4% of the time, Pallas kernels for 0%

commit v1 on v0

v1 whole, which is shorter than its diff:
```python
import jax
import jax.numpy as jnp
from jax import lax
from jax.experimental import pallas as pl
from jax.experimental.pallas import tpu as pltpu
from jax.sharding import PartitionSpec as P

STATE = 128
SPAN = 128
LANES = 128
HB = 8
F32 = jnp.float32
BF16 = jnp.bfloat16
INTERPRET = False


def span_layout(episode_spans, last_valid, first_span, span_count):
    span_ids = first_span + jnp.arange(span_count, dtype=jnp.int32)
    starts = jnp.cumsum(episode_spans) - episode_spans
    finals = starts + episode_spans - 1
    resets = jnp.any(span_ids[:, None] == starts[None, :], axis=1)
    final_hit = span_ids[:, None] == finals[None, :]
    valid_count = jnp.sum(jnp.where(final_hit, last_valid[None, :] - SPAN, 0), axis=1) + SPAN
    offsets = jnp.arange(SPAN, dtype=jnp.int32)
    valid_mask = jnp.where(offsets[None, :] < valid_count[:, None], 1.0, 0.0).astype(F32)
    keep_flag = jnp.where(resets, 0.0, 1.0).astype(F32)
    return (valid_mask, keep_flag)


def dot(a, b, ca, cb):
    return lax.dot_general(a, b, (((ca,), (cb,)), ((), ())), preferred_element_type=F32)


def first_lanes(feat):
    return lax.broadcasted_iota(jnp.int32, (SPAN, LANES), 1) < feat


def state_kernel(x_ref, w_ref, b_ref, fac_ref, s_ref, total_ref, run_ref):
    k = pl.program_id(1)
    feat = x_ref.shape[1] // HB
    low = first_lanes(feat)
    b = b_ref[...]
    w = w_ref[0, 0]

    @pl.when(k == 0)
    def _():
        run_ref[...] = jnp.zeros_like(run_ref)

    for j in range(HB // 2):
        sl = slice(j * LANES, (j + 1) * LANES)
        w2 = jnp.where(low, w[:, 2 * j : 2 * j + 1], w[:, 2 * j + 1 : 2 * j + 2])
        weighted = (x_ref[:, sl].astype(F32) * w2).astype(BF16)
        state = dot(weighted, b, 0, 0)
        s_ref[0, sl, :] = state
        for i in range(2):
            rows = slice(i * feat, (i + 1) * feat)
            at = slice(j * LANES + i * feat, j * LANES + (i + 1) * feat)
            h = 2 * j + i
            run_ref[at, :] = run_ref[at, :] * fac_ref[0, h : h + 1, :] + state[rows]
    total_ref[...] = run_ref[...].astype(BF16)


def out_kernel(
    x_ref, dy_ref, valid_ref, b_ref, c_ref, ent_ref, col_ref, row_ref, srow_ref, fac_ref,
    keep_ref, skip_ref,
    dx_ref, term_ref, total_ref, dcol_ref, dsrow_ref, skip_out_ref, db_ref, dc_ref,
    run_ref, dg_ref,
):
    hb, step = pl.program_id(0), pl.program_id(1)
    k = pl.num_programs(1) - 1 - step
    feat = x_ref.shape[1] // HB
    low = first_lanes(feat)
    b, c = b_ref[...], c_ref[...]
    scores = dot(c, b, 1, 1)
    causal = lax.broadcasted_iota(jnp.int32, (SPAN, SPAN), 0) >= lax.broadcasted_iota(
        jnp.int32, (SPAN, SPAN), 1
    )
    col = col_ref[0, 0]
    grown = jnp.exp(col)
    keep = keep_ref[0, 0:1, :]
    valid = jnp.broadcast_to(valid_ref[0], (SPAN, LANES))

    @pl.when(step == 0)
    def _():
        run_ref[...] = jnp.zeros_like(run_ref)

    @pl.when(hb == 0)
    def _():
        dg_ref[k] = jnp.zeros((SPAN, SPAN), F32)
        dc_ref[k] = jnp.zeros((SPAN, STATE), F32)

    dg = jnp.zeros((SPAN, SPAN), F32)
    dc = jnp.zeros((SPAN, STATE), F32)
    dcol = jnp.zeros((SPAN, HB), F32)
    lane = lax.broadcasted_iota(jnp.int32, (SPAN, HB), 1)
    for j in range(HB // 2):
        sl = slice(j * LANES, (j + 1) * LANES)
        x2 = x_ref[:, sl]
        dyf = dy_ref[:, sl].astype(F32) * valid
        dy2 = dyf.astype(BF16)
        e2 = ent_ref[0, sl, :]
        ec2 = jnp.where(low, grown[:, 2 * j : 2 * j + 1], grown[:, 2 * j + 1 : 2 * j + 2])
        dkf = dyf * ec2
        dk2 = dkf.astype(BF16)
        q2 = dkf * dot(c, e2, 1, 1)
        term = dot(dk2, c, 0, 0) * keep
        term_ref[0, sl, :] = term
        dc = dc + dot(dk2, e2, 1, 0)
        skip_out_ref[0, 0, j : j + 1, :] = jnp.sum(dyf * x2.astype(F32), axis=0, keepdims=True)
        dx = skip_ref[:, sl] * dyf
        for i in range(2):
            h = 2 * j + i
            mine = low if i == 0 else jnp.logical_not(low)
            dyi = jnp.where(mine, dyf, 0.0).astype(BF16)
            s_row = srow_ref[0, h : h + 1, :]
            gap = jnp.where(causal, col[:, h : h + 1] - row_ref[0, h : h + 1, :], -jnp.inf)
            decay = jnp.exp(gap)
            mixing = (decay * scores * s_row).astype(BF16)
            dm = dot(dyi, x2, 1, 1).astype(BF16).astype(F32)
            t1 = dm * decay
            dg = dg + t1 * s_row
            t2 = t1 * scores
            dsrow_ref[0, h : h + 1, :] = jnp.sum(t2, axis=0, keepdims=True)
            summed = jnp.sum(t2 * s_row + jnp.where(mine, q2, 0.0), axis=1, keepdims=True)
            dcol = jnp.where(lane == h, summed, dcol)
            dx = dx + dot(mixing, dyi, 0, 0)
            at = slice(j * LANES + i * feat, j * LANES + (i + 1) * feat)
            run_ref[at, :] = (
                run_ref[at, :] * fac_ref[0, h : h + 1, :] + term[i * feat : (i + 1) * feat]
            )
        dx_ref[:, sl] = dx.astype(BF16)
    skip_out_ref[0, 0, HB // 2 :, :] = jnp.zeros((HB - HB // 2, LANES), F32)
    dcol_ref[0, 0] = dcol
    dg_ref[k] = dg_ref[k] + dg
    dc_ref[k] = dc_ref[k] + dc
    total_ref[...] = run_ref[...].astype(BF16)

    @pl.when(hb == pl.num_programs(0) - 1)
    def _():
        low_dg = dg_ref[k].astype(BF16)
        dc_ref[k] = dc_ref[k] + dot(low_dg, b, 1, 0)
        db_ref[k] = dot(low_dg, c, 0, 0)


def end_kernel(
    x_ref, w_ref, b_ref, after_ref, term_ref, ent_ref, fac_ref, dx1_ref,
    dx_ref, dw_ref, dcot_ref, db_ref,
    carry_ref,
):
    hb, step = pl.program_id(0), pl.program_id(1)
    k = pl.num_programs(1) - 1 - step
    feat = x_ref.shape[1] // HB
    low = first_lanes(feat)
    b = b_ref[...]
    w = w_ref[0, 0]

    @pl.when(step == 0)
    def _():
        carry_ref[...] = after_ref[...].astype(F32)

    @pl.when(hb == 0)
    def _():
        db_ref[k] = jnp.zeros((SPAN, STATE), F32)

    db = jnp.zeros((SPAN, STATE), F32)
    dw = jnp.zeros((SPAN, HB), F32)
    lane = lax.broadcasted_iota(jnp.int32, (SPAN, HB), 1)
    for j in range(HB // 2):
        sl = slice(j * LANES, (j + 1) * LANES)
        ds = carry_ref[sl, :]
        ds_low = ds.astype(BF16)
        xf = x_ref[:, sl].astype(F32)
        w2 = jnp.where(low, w[:, 2 * j : 2 * j + 1], w[:, 2 * j + 1 : 2 * j + 2])
        db = db + dot((xf * w2).astype(BF16), ds_low, 1, 0)
        dweighted = dot(b, ds_low, 1, 1).astype(BF16).astype(F32)
        dx_ref[:, sl] = (dx1_ref[:, sl].astype(F32) + dweighted * w2).astype(BF16)
        part = dweighted * xf
        met = ds * ent_ref[0, sl, :].astype(F32)
        for i in range(2):
            h = 2 * j + i
            mine = low if i == 0 else jnp.logical_not(low)
            summed = jnp.sum(jnp.where(mine, part, 0.0), axis=1, keepdims=True)
            dw = jnp.where(lane == h, summed, dw)
            rows = slice(i * feat, (i + 1) * feat)
            dcot_ref[0, h : h + 1, :] = jnp.sum(met[rows], axis=0, keepdims=True)
            at = slice(j * LANES + i * feat, j * LANES + (i + 1) * feat)
            carry_ref[at, :] = ds[rows] * fac_ref[0, h : h + 1, :] + term_ref[0, at, :]
    dw_ref[0, 0] = dw
    db_ref[k] = db_ref[k] + db


def scan_heads(total, factor_all, axis, reverse):
    count = lax.axis_size(axis)
    rows, width = total.shape
    feat = rows // factor_all.shape[1]
    mine = lax.all_to_all(total.reshape(count, rows // count, width), axis, 0, 0)
    own = factor_all.shape[1] // count
    here = lax.dynamic_slice_in_dim(factor_all, lax.axis_index(axis) * own, own, axis=1)
    here = jnp.repeat(here, feat, axis=1)[:, :, None]
    running = jnp.zeros(mine.shape[1:], F32)
    before = [None] * count
    for at in reversed(range(count)) if reverse else range(count):
        before[at] = running.astype(BF16)
        running = here[at] * running + mine[at].astype(F32)
    return lax.all_to_all(jnp.stack(before), axis, 0, 0).reshape(rows, width)


def shards(
    activations,
    head_inputs,
    out_cotangent,
    episode_spans,
    last_valid,
    mixer_weight,
    step_weight,
    decay_log,
    step_bias,
    skip_gain,
):
    token_rows = activations[0]
    x = head_inputs[0]
    dy = out_cotangent[0]
    tokens, hp = x.shape
    spans = tokens // SPAN
    heads = decay_log.shape[0]
    feat = hp // heads
    blocks = heads // HB
    wide = HB * feat
    first_span = lax.axis_index("shard") * spans
    valid, keep = span_layout(episode_spans[0], last_valid[0], first_span, spans)
    joined = jnp.concatenate([mixer_weight, step_weight], axis=1)
    gathered = lax.all_gather(joined, "shard", axis=0, tiled=True)
    projected = jnp.dot(token_rows, gathered, preferred_element_type=F32)
    b_map = projected[:, :STATE].astype(BF16)
    c_map = projected[:, STATE : 2 * STATE].astype(BF16)
    raw = (projected[:, 2 * STATE :] + step_bias[None, :]).reshape(spans, SPAN, heads)
    rate = -jnp.exp(decay_log)
    steps = jax.nn.softplus(raw) * valid[:, :, None]
    tri = jnp.tril(jnp.ones((SPAN, SPAN), F32))
    exact = lax.Precision.HIGHEST
    cum = jnp.einsum("ts,ksh->kth", tri, steps * rate, precision=exact)
    last = cum[:, -1:, :]
    tail = jnp.exp(last - cum)
    weights = tail * steps
    decays = jnp.exp(last[:, 0])
    factors = decays * keep[:, None]
    factor_all = lax.all_gather(jnp.prod(factors, axis=0), "shard")

    def columns(a):
        return a.reshape(spans, SPAN, blocks, HB).transpose(0, 2, 1, 3)

    def from_columns(a):
        return a.transpose(0, 2, 1, 3).reshape(spans, SPAN, heads)

    w_cols, c_cols = columns(weights), columns(cum)
    c_rows, s_rows = cum.transpose(0, 2, 1), steps.transpose(0, 2, 1)
    fac_rows = jnp.broadcast_to(factors[:, :, None], (spans, heads, LANES))
    keep_rows = jnp.broadcast_to(keep[:, None, None], (spans, 8, LANES))
    skip_lanes = jnp.repeat(skip_gain, feat)[None, :]

    def specs(order):
        return {
            "tok": pl.BlockSpec((SPAN, wide), lambda h, k: (order(k), h)),
            "col": pl.BlockSpec((1, 1, SPAN, HB), lambda h, k: (order(k), h, 0, 0)),
            "row": pl.BlockSpec((1, HB, LANES), lambda h, k: (order(k), h, 0)),
            "map": pl.BlockSpec((SPAN, STATE), lambda h, k: (order(k), 0)),
            "state": pl.BlockSpec((1, wide, STATE), lambda h, k: (order(k), h, 0)),
            "total": pl.BlockSpec((wide, STATE), lambda h, k: (h, 0)),
            "valid": pl.BlockSpec((1, SPAN, 1), lambda h, k: (order(k), 0, 0)),
            "keep": pl.BlockSpec((1, 8, LANES), lambda h, k: (order(k), 0, 0)),
            "skip": pl.BlockSpec((1, wide), lambda h, k: (0, h)),
            "skipout": pl.BlockSpec((1, 1, HB, LANES), lambda h, k: (order(k), h, 0, 0)),
            "whole": pl.BlockSpec((spans, SPAN, STATE), lambda h, k: (0, 0, 0)),
        }

    up, down = specs(lambda k: k), specs(lambda k: spans - 1 - k)
    shape = jax.ShapeDtypeStruct
    state_shape = shape((spans, hp, STATE), F32)
    total_shape = shape((hp, STATE), BF16)
    col_shape = shape((spans, blocks, SPAN, HB), F32)
    row_shape = shape((spans, heads, LANES), F32)
    whole_shape = shape((spans, SPAN, STATE), F32)

    states, total = pl.pallas_call(
        state_kernel,
        grid=(blocks, spans),
        in_specs=[up[n] for n in ("tok", "col", "map", "row")],
        out_specs=[up[n] for n in ("state", "total")],
        out_shape=[state_shape, total_shape],
        scratch_shapes=[pltpu.VMEM((wide, STATE), F32)],
        interpret=INTERPRET,
        name="span_states",
    )(x, w_cols, b_map, fac_rows)

    carry = scan_heads(total, factor_all, "shard", False).astype(F32)
    entering = []
    for k in range(spans):
        entering.append((carry * keep[k]).astype(BF16))
        if k + 1 < spans:
            carry = jnp.repeat(factors[k], feat)[:, None] * carry + states[k]
    entering = jnp.stack(entering)

    dx1, terms, back_total, dcols, ds_rows, skip_rows, db1, dc_map = pl.pallas_call(
        out_kernel,
        grid=(blocks, spans),
        in_specs=[
            down[n]
            for n in (
                "tok", "tok", "valid", "map", "map", "state", "col", "row", "row", "row",
                "keep", "skip",
            )
        ],
        out_specs=[
            down[n]
            for n in ("tok", "state", "total", "col", "row", "skipout", "whole", "whole")
        ],
        out_shape=[
            shape((tokens, hp), BF16),
            state_shape,
            total_shape,
            col_shape,
            row_shape,
            shape((spans, blocks, HB, LANES), F32),
            whole_shape,
            whole_shape,
        ],
        scratch_shapes=[
            pltpu.VMEM((wide, STATE), F32),
            pltpu.VMEM((spans, SPAN, SPAN), F32),
        ],
        interpret=INTERPRET,
        name="span_out_back",
    )(
        x, dy, valid[:, :, None], b_map, c_map, entering, c_cols, c_rows, s_rows, fac_rows,
        keep_rows, skip_lanes,
    )

    after = scan_heads(back_total, factor_all, "shard", True)
    dx, dw_cols, dcot_rows, db2 = pl.pallas_call(
        end_kernel,
        grid=(blocks, spans),
        in_specs=[
            down[n] for n in ("tok", "col", "map", "total", "state", "state", "row", "tok")
        ],
        out_specs=[down[n] for n in ("tok", "col", "row", "whole")],
        out_shape=[shape((tokens, hp), BF16), col_shape, row_shape, whole_shape],
        scratch_shapes=[pltpu.VMEM((wide, STATE), F32)],
        interpret=INTERPRET,
        name="span_end_back",
    )(x, w_cols, b_map, after, terms, entering, fac_rows, dx1)

    decay_cot = jnp.sum(dcot_rows, axis=2)
    dw = from_columns(dw_cols)
    ds_in = ds_rows.transpose(0, 2, 1)
    dww = dw * weights
    dcum = from_columns(dcols) - steps * ds_in - dww
    at_last = jnp.sum(dww, axis=1) + decay_cot * decays
    da = jnp.einsum("ts,kth->ksh", tri, dcum, precision=exact) + at_last[:, None, :]
    dsteps = ds_in + dw * tail + da * rate
    decay_local = jnp.sum(da * steps, axis=(0, 1)) * rate
    raw_cot = dsteps * valid[:, :, None] * jax.nn.sigmoid(raw)
    skip_local = jnp.sum(
        skip_rows[:, :, : HB // 2].reshape(spans, heads, feat), axis=(0, 2)
    )
    db = (db1 + db2).astype(BF16).reshape(tokens, STATE)
    joined_cot = jnp.concatenate(
        [db, dc_map.astype(BF16).reshape(tokens, STATE), raw_cot.astype(BF16).reshape(tokens, -1)],
        axis=1,
    )
    grads_local = lax.dot_general(
        token_rows, joined_cot, (((0,), (0,)), ((), ())), preferred_element_type=F32
    )
    shared = lax.psum_scatter(grads_local.astype(BF16), "shard", scatter_dimension=0, tiled=True)
    back_rows = lax.dot_general(
        joined_cot, gathered, (((1,), (1,)), ((), ())), preferred_element_type=F32
    )
    summed = lax.psum(shared, "replica").astype(F32)
    small = lax.psum(
        jnp.stack([decay_local, jnp.sum(raw_cot, axis=(0, 1)), skip_local]),
        ("replica", "shard"),
    )
    return (
        dx[None],
        back_rows.astype(BF16)[None],
        summed[:, : 2 * STATE],
        summed[:, 2 * STATE :],
        small[0],
        small[1],
        small[2],
    )


def solution(mesh):
    return jax.shard_map(
        shards,
        mesh=mesh,
        in_specs=(
            P("replica", "shard", None),
            P("replica", "shard", None),
            P("replica", "shard", None),
            P("replica", None),
            P("replica", None),
            P("shard", None),
            P("shard", None),
            P(),
            P(),
            P(),
        ),
        out_specs=(
            P("replica", "shard", None),
            P("replica", "shard", None),
            P("shard", None),
            P("shard", None),
            P(),
            P(),
            P(),
        ),
        check_vma=False,
    )
```

time: 566 us -> 317 us (0.56)
  other arithmetic: 171 us -> 25.4 us
  local copies, waits for them, and re-layouts: 112 us -> 20.2 us
  Pallas kernels: 0 us -> 62.5 us
  waiting for transfers between devices: 148 us -> 109 us
  matrix products: 48.8 us -> 10.7 us
  starting transfers between devices: 0.21 us -> 14.4 us
  blocking collectives: 66.8 us -> 58.9 us
    all_gather x2 -> x0, waiting for transfers between devices: 75.5 us -> none  [entering_2(): lax.all_gather(part.astype(kind), axis)]
    pallas_call x0 -> x3, Pallas kernels: none -> 62.5 us  [the longest x1 32 us: shards(): pl.pallas_call(out_kernel, grid=(blocks, spans), in_specs=[down[n] for n...]
    select_n x18 -> x3, other arithmetic: 55.8 us -> 0.81 us  [the longest x2 0.8 us: span_layout(): jnp.where(offsets[None, :] < valid_count[:, None], 1.0, 0.0).astype(F32)]
    reduce_scatter x1, waiting for transfers between devices: 43.6 us -> 2.82 us  [shards(): lax.psum_scatter(grads_local.astype(BF16), 'shard', scatter_dimension=0,...]
    all_to_all x0 -> x4, waiting for transfers between devices: none -> 40.6 us  [the longest x2 25.5 us: scan_heads(): return lax.all_to_all(jnp.stack(before), axis, 0, 0).reshape(rows, width)]
    dot_general x23 -> x3, matrix products: 41.9 us -> 3.86 us  [the longest x1 3.18 us: shards(): projected = jnp.dot(token_rows, gathered, preferred_element_type=F32)]
    psum x1, waiting for transfers between devices: 0.01 us -> 33.4 us  [shards(): summed = lax.psum(shared, 'replica').astype(F32)]
    add x11 -> x2, other arithmetic: 32.1 us -> 0.19 us  [the longest x1 0.18 us: shards(): at_last = jnp.sum(dww, axis=1) + decay_cot * decays]
  transfers between devices with their start and end apart: 5 -> 7, of which waited for: 4 -> 6; matrix products, arithmetic and copies ran while one was open for 4% -> 5% of each run, Pallas kernels for 0% -> 0%
where the time goes in v1:
time: 317 us; the launch traced here: 316 us
  waiting for transfers between devices  109 us (34%)
  Pallas kernels  62.5 us (20%)
  blocking collectives  58.9 us (19%)
  other arithmetic  25.4 us (8%)
  local copies, waits for them, and re-layouts  20.2 us (6%)
  between operations  14.7 us (5%)
  starting transfers between devices  14.4 us (5%)
  matrix products  10.7 us (3%)
    psum x1, blocking collectives, shards(): lax.psum(jnp.stack([decay_local, jnp.sum(raw_cot, axis=(0, 1)), skip_loca...  39.3 us
    psum x1, waiting for transfers between devices, shards(): summed = lax.psum(shared, 'replica').astype(F32)  33.4 us
    pallas_call x1, Pallas kernels, shards(): pl.pallas_call(out_kernel, grid=(blocks, spans), in_specs=[down[n] for n...  32 us
    all_gather x1, waiting for transfers between devices, shards(): gathered = lax.all_gather(joined, 'shard', axis=0, tiled=True)  32 us
    all_to_all x2, waiting for transfers between devices, scan_heads(): return lax.all_to_all(jnp.stack(before), axis, 0, 0).reshape(rows, width)  25.5 us
    unnamed x1, blocking collectives  19.6 us
    pallas_call x1, Pallas kernels, shards(): pl.pallas_call(end_kernel, grid=(blocks, spans), in_specs=[down[n] for n...  16.6 us
    all_to_all x2, waiting for transfers between devices, scan_heads(): lax.all_to_all(total.reshape(count, rows // count, width), axis, 0, 0)  15.2 us
  transfers between devices with their start and end apart: 7, of which 6 were waited for; matrix products, arithmetic and copies ran while one was open for 5% of the time, Pallas kernels for 0%

profile of v1, /device:TPU:0, one launch (start us, length us, event | category | flops | bytes accessed | tf_op | source)
XLA Modules:
  0.0 315.8 jit_solution(11019767462193319380)
XLA Ops:
  7.2 1.1 copy.64
  8.3 1.7 pad_maximum_fusion.1
  10.1 0.8 reduce-window.4
  13.4 32.0 %all-gather.3.cloned.1.call-done = bf16[4096,320]{1,0:T(8,128)(2,1)} async-done(((bf16[512,320]{1,0:T(8,128)(2,1)}), bf16[4096,320]{1,0:T(8,128)(2,1)}) %all-gather.3.cloned.1.call-update) | async-done | bytes 2621456 | tf_op jit(solution)/shard_map/all_gather | solution.py:232
  45.4 3.2 %fusion.71 = (bf16[256,320]{1,0:T(8,128)(2,1)S(1)}, f32[256,320]{1,0:T(8,128)S(1)}) fusion(bf16[4096,320]{1,0:T(8,128)(2,1)} %all-gather.3.cloned.1.call-done, bf16[1,256,4096]{2,1,0:T(8,128)(2,1)S(1)} %copy-done), kind=kOutput, calls=%fused_computation.132 | convolution fusion | flops 671170560 | bytes 5210112 | tf_op jit(solution)/shard_map/dot_general | solution.py:233
  50.6 1.3 copy.71
  51.9 0.7 broadcast_in_dim.134.fac_ref
  52.6 13.9 %span_states.1 = (f32[2,4096,128]{2,1,0:T(8,128)}, bf16[4096,128]{1,0:T(8,128)(2,1)}) custom-call(bf16[256,4096]{1,0:T(8,128)(2,1)} %bitcast.141, f32[2,8,128,8]{3,2,1,0:T(8,128)} %bitcast.144, bf16[256,128]{1,0:T(8,128)(2,1)} %get-tuple-element.74.b_ref, f32[2,64,128]{2,1,0:T(8,128)} %broadcast_in_dim.134.fac_ref), custom_call_target="tpu_custom_call" | custom-call | tf_op jit(solution)/shard_map/span_states/pallas_call | solution.py:284
  66.5 3.6 %all-to-all-start = ((bf16[8,512,128]{2,1,0:T(8,128)(2,1)}), bf16[8,512,128]{2,1,0:T(8,128)(2,1)S(1)}, u32[]{:S(2)}, u32[]{:S(2)}) async-start(bf16[8,512,128]{2,1,0:T(8,128)(2,1)} %bitcast.153), calls=%async_computation | async-start | bytes 2097152 | tf_op jit(solution)/shard_map/all_to_all | solution.py:196
  72.2 19.6 %all-reduce.1 = f32[8,64]{1,0:T(8,128)S(1)} all-reduce(f32[8,64]{1,0:T(8,128)S(1)} %reshape.603), channel_id=2, replica_groups=mesh['replica'=4,'shard'=8] {'shard'}, use_global_device_ids=true, to_apply=%add | all-reduce | flops 512 | bytes 4096
  92.9 0.8 fusion.27
  93.7 0.9 fusion.26
  94.6 0.9 convert_dynamic-update-slice_fusion.3
  95.5 1.0 fusion.24
  96.5 1.1 convert_dynamic-update-slice_fusion.2
  97.6 0.8 fusion.23
  98.4 0.9 fusion.28
  99.2 3.6 %all-to-all-start.1 = ((bf16[8,512,128]{2,1,0:T(8,128)(2,1)}), bf16[8,512,128]{2,1,0:T(8,128)(2,1)S(1)}, u32[]{:S(2)}, u32[]{:S(2)}) async-start(bf16[8,512,128]{2,1,0:T(8,128)(2,1)} %fusion.28), calls=%async_computation.1 | async-start | bytes 2097152 | tf_op jit(solution)/shard_map/all_to_all | solution.py:205
  104.1 0.7 fusion.31.valid_ref
  105.0 1.3 copy.72
  106.4 11.7 %all-to-all-done.1 = bf16[8,512,128]{2,1,0:T(8,128)(2,1)S(1)} async-done(((bf16[8,512,128]{2,1,0:T(8,128)(2,1)}), bf16[8,512,128]{2,1,0:T(8,128)(2,1)S(1)}, u32[]{:S(2)}, u32[]{:S(2)}) %all-to-all-start.1) | async-done | bytes 1048608 | tf_op jit(solution)/shard_map/all_to_all | solution.py:205
  118.1 3.4 %fusion.2 = (bf16[1,4096,128]{2,1,0:T(8,128)(2,1)S(1)}, bf16[1,4096,128]{2,1,0:T(8,128)(2,1)S(1)}) fusion(f32[]{:T(128)} %bitcast.25, f32[]{:T(128)} %bitcast.28, f32[2,4096,128]{2,1,0:T(8,128)} %get-tuple-element.22, f32[4096]{0:T(1024)S(1)} %mul.298, bf16[1,4096,128]{2,1,0:T(8,128)(2,1)S(1)} %bitcast.148), kind=kLoop, calls=%fused_computation.6 | loop fusion | flops 3670016 | bytes 5259272 | tf_op jit(solution)/shard_map/convert_element_type | solution.py:298
  121.5 1.5 pad_maximum_fusion.ent_ref
  123.6 32.0 %span_out_back.1 = (bf16[256,4096]{1,0:T(8,128)(2,1)}, f32[2,4096,128]{2,1,0:T(8,128)}, bf16[4096,128]{1,0:T(8,128)(2,1)}, f32[2,8,128,8]{3,2,1,0:T(8,128)}, f32...) custom-call(bf16[256,4096]{1,0:T(8,128)(2,1)} %bitcast.142, ...), custom_call_target="tpu_custom_call" | custom-call | tf_op jit(solution)/shard_map/span_out_back/pallas_call | solution.py:303
  155.7 3.6 %all-to-all-start.2 = ((bf16[8,512,128]{2,1,0:T(8,128)(2,1)}), bf16[8,512,128]{2,1,0:T(8,128)(2,1)S(1)}, u32[]{:S(2)}, u32[]{:S(2)}) async-start(bf16[8,512,128]{2,1,0:T(8,128)(2,1)} %bitcast.155), calls=%async_computation.2 | async-start | bytes 2097152 | tf_op jit(solution)/shard_map/all_to_all | solution.py:196
  159.4 15.2 %all-to-all-done.2 = bf16[8,512,128]{2,1,0:T(8,128)(2,1)S(1)} async-done(((bf16[8,512,128]{2,1,0:T(8,128)(2,1)}), bf16[8,512,128]{2,1,0:T(8,128)(2,1)S(1)}, u32[]{:S(2)}, u32[]{:S(2)}) %all-to-all-start.2) | async-done | bytes 1048608 | tf_op jit(solution)/shard_map/all_to_all | solution.py:196
  174.6 1.2 fusion.30
  175.8 0.8 fusion.21
  177.2 1.0 fusion.22
  178.2 0.9 convert_dynamic-update-slice_fusion
  179.2 0.9 fusion.25
  180.0 0.8 fusion.29
  181.5 3.6 %all-to-all-start.3 = ((bf16[8,512,128]{2,1,0:T(8,128)(2,1)}), bf16[8,512,128]{2,1,0:T(8,128)(2,1)S(1)}, u32[]{:S(2)}, u32[]{:S(2)}) async-start(bf16[8,512,128]{2,1,0:T(8,128)(2,1)} %broadcast_dynamic-update-slice_fusion), calls=%async_computation.3 | async-start | bytes 2097152 | tf_op jit(solution)/shard_map/all_to_all | solution.py:205
  185.1 1.5 copy.74
  186.7 13.7 %all-to-all-done.3 = bf16[8,512,128]{2,1,0:T(8,128)(2,1)S(1)} async-done(((bf16[8,512,128]{2,1,0:T(8,128)(2,1)}), bf16[8,512,128]{2,1,0:T(8,128)(2,1)S(1)}, u32[]{:S(2)}, u32[]{:S(2)}) %all-to-all-start.3) | async-done | bytes 1048608 | tf_op jit(solution)/shard_map/all_to_all | solution.py:205
  200.4 1.0 copy-done.1
  201.3 16.6 %span_end_back.1 = (bf16[256,4096]{1,0:T(8,128)(2,1)}, f32[2,8,128,8]{3,2,1,0:T(8,128)}, f32[2,64,128]{2,1,0:T(8,128)}, f32[2,128,128]{2,1,0:T(8,128)}) custom-call(bf16[256,4096]{1,0:T(8,128)(2,1)} %bitcast.143, f32[2,8,128,8]{3,2,1,0:T(8,128)} %bitcast.145, bf16[256,128]{1,0:T(8,128)(2,1)} %get-tuple-element.74.b_ref, bf16[4096,128]{1,0:T(8,128)(2,1)} %bitcast.147, ...), custom_call_target="tpu_custom_call" | custom-call | tf_op jit(solution)/shard_map/span_end_back/pallas_call | solution.py:339
  218.0 1.0 reduce_sum.68
  219.1 1.5 copy.73
  221.7 2.4 fusion
  224.1 0.8 copy-done.7
  225.1 39.3 %psum.15 = f32[3,64]{1,0:T(4,128)S(1)} all-reduce(f32[3,64]{1,0:T(4,128)S(1)} %pad_maximum_fusion.5), channel_id=1, replica_groups=mesh['replica'=4,'shard'=8] {'replica','shard'}, use_global_device_ids=true, to_apply=%region_12.13 | all-reduce | flops 192 | bytes 1536 | tf_op jit(solution)/shard_map/psum | solution.py:378
  264.5 2.8 reduce-scatter.2.cloned.1.call-done
  267.8 4.5 %fusion.1 = bf16[1,256,4096]{2,1,0:T(8,128)(2,1)} fusion(bf16[4096,320]{1,0:T(8,128)(2,1)} %all-gather.3.cloned.1.call-done, bf16[256,64]{1,0:T(8,128)(2,1)S(1)} %bitcast.162, bf16[256,128]{1,0:T(8,128)(2,1)S(1)} %bitcast.158, bf16[256,128]{1,0:T(8,128)(2,1)S(1)} %bitcast.160), kind=kOutput, calls=%fused_computation.3 | convolution fusion | flops 672628736 | bytes 4882432 | tf_op jit(solution)/shard_map/dot_general | solution.py:374
  272.3 33.4 %all-reduce.4.cloned.1.call-done = bf16[512,320]{0,1:T(8,128)(2,1)} async-done(((bf16[512,320]{0,1:T(8,128)(2,1)}), bf16[512,320]{0,1:T(8,128)(2,1)}) %all-reduce.4.cloned.1.call-update) | async-done | bytes 327696 | tf_op jit(solution)/shard_map/psum | solution.py:377
  305.7 1.0 slice.204
  306.7 1.0 copy.80
  307.7 1.5 slice.205
  (94 shorter events, 12.7 us)
Async XLA Ops:
  7.2 38.2 %copy-start = (bf16[1,256,4096]{2,1,0:T(8,128)(2,1)S(1)}, bf16[1,256,4096]{2,1,0:T(8,128)(2,1)}, u32[]{:S(2)}) copy-start(bf16[1,256,4096]{2,1,0:T(8,128)(2,1)} %param.10) | copy-start | bytes 6291460
  7.2 38.2 %all-gather.3.cloned.1.call-start = ((), (), s32[]{:S(2)}) async-start(), calls=%async_computation.5 | async-start | bytes 3538944 | tf_op jit(solution)/shard_map/all_gather | solution.py:232
  13.4 35.9 %copy-start.8 = (f32[64]{0:T(128)S(1)}, f32[64]{0:T(128)}, u32[]{:S(2)}) copy-start(f32[64]{0:T(128)} %param.18) | copy-start | bytes 772
  49.6 55.4 %copy-start.2 = (f32[2,64,128]{2,1,0:T(8,128)}, f32[2,64,128]{2,1,0:T(8,128)S(1)}, u32[]{:S(2)}) copy-start(f32[2,64,128]{2,1,0:T(8,128)S(1)} %fusion.40.row_ref) | copy-start | bytes 196612
  52.6 17.5 %copy-start.12 = (u32[32]{0:T(128)S(1)}, u32[32]{0:T(128)}, u32[]{:S(2)}) copy-start(u32[32]{0:T(128)} %constant.45) | copy-start | bytes 388
  66.5 26.5 %all-to-all-start = ((bf16[8,512,128]{2,1,0:T(8,128)(2,1)}), bf16[8,512,128]{2,1,0:T(8,128)(2,1)S(1)}, u32[]{:S(2)}, u32[]{:S(2)}) async-start(bf16[8,512,128]{2,1,0:T(8,128)(2,1)} %bitcast.153), calls=%async_computation | async-start | bytes 2097152 | tf_op jit(solution)/shard_map/all_to_all | solution.py:196
  96.5 6.3 %copy-start.9 = (f32[64]{0:T(128)S(1)}, f32[64]{0:T(128)}, u32[]{:S(2)}) copy-start(f32[64]{0:T(128)} %param.19) | copy-start | bytes 772
  99.2 18.9 %all-to-all-start.1 = ((bf16[8,512,128]{2,1,0:T(8,128)(2,1)}), bf16[8,512,128]{2,1,0:T(8,128)(2,1)S(1)}, u32[]{:S(2)}, u32[]{:S(2)}) async-start(bf16[8,512,128]{2,1,0:T(8,128)(2,1)} %fusion.28), calls=%async_computation.1 | async-start | bytes 2097152 | tf_op jit(solution)/shard_map/all_to_all | solution.py:205
  155.7 18.9 %all-to-all-start.2 = ((bf16[8,512,128]{2,1,0:T(8,128)(2,1)}), bf16[8,512,128]{2,1,0:T(8,128)(2,1)S(1)}, u32[]{:S(2)}, u32[]{:S(2)}) async-start(bf16[8,512,128]{2,1,0:T(8,128)(2,1)} %bitcast.155), calls=%async_computation.2 | async-start | bytes 2097152 | tf_op jit(solution)/shard_map/all_to_all | solution.py:196
  177.2 7.9 %copy-start.4 = (f32[2,128,128]{2,1,0:T(8,128)S(1)}, f32[2,128,128]{2,1,0:T(8,128)}, u32[]{:S(2)}) copy-start(f32[2,128,128]{2,1,0:T(8,128)} %get-tuple-element.29) | copy-start | bytes 393220
  181.5 18.9 %all-to-all-start.3 = ((bf16[8,512,128]{2,1,0:T(8,128)(2,1)}), bf16[8,512,128]{2,1,0:T(8,128)(2,1)S(1)}, u32[]{:S(2)}, u32[]{:S(2)}) async-start(bf16[8,512,128]{2,1,0:T(8,128)(2,1)} %broadcast_dynamic-update-slice_fusion), calls=%async_computation.3 | async-start | bytes 2097152 | tf_op jit(solution)/shard_map/all_to_all | solution.py:205
  185.1 82.2 %reduce-scatter.2.cloned.1.call-start = ((), (), s32[]{:S(2)}) async-start(), calls=%async_computation.6 | async-start | bytes 2949120 | tf_op jit(solution)/shard_map/reduce_scatter | solution.py:373
  200.4 1.0 copy-start.1
  201.3 19.3 %copy-start.3 = (f32[2,64,128]{2,1,0:T(8,128)S(1)}, f32[2,64,128]{2,1,0:T(8,128)}, u32[]{:S(2)}) copy-start(f32[2,64,128]{2,1,0:T(8,128)} %copy-done.2) | copy-start | bytes 196612
  201.3 19.8 %copy-start.10 = (f32[2,64,128]{2,1,0:T(8,128)S(1)}, f32[2,64,128]{2,1,0:T(8,128)}, u32[]{:S(2)}) copy-start(f32[2,64,128]{2,1,0:T(8,128)} %get-tuple-element.30) | copy-start | bytes 196612
  218.0 3.7 %copy-start.5 = (f32[2,128,128]{2,1,0:T(8,128)S(1)}, f32[2,128,128]{2,1,0:T(8,128)}, u32[]{:S(2)}) copy-start(f32[2,128,128]{2,1,0:T(8,128)} %get-tuple-element.27) | copy-start | bytes 393220
  218.0 3.7 %copy-start.6 = (f32[2,128,128]{2,1,0:T(8,128)S(1)}, f32[2,128,128]{2,1,0:T(8,128)}, u32[]{:S(2)}) copy-start(f32[2,128,128]{2,1,0:T(8,128)} %get-tuple-element.28) | copy-start | bytes 393220
  224.1 0.8 copy-start.7
  224.1 1.0 copy-start.11
  224.1 81.6 %all-reduce.4.cloned.1.call-start = ((), (), s32[]{:S(2)}) async-start(), calls=%async_computation.7 | async-start | bytes 655360 | tf_op jit(solution)/shard_map/psum | solution.py:377
Sparse Core Ops, SparseCore 0:
  10.4 34.8 all-gather.2
  224.2 43.0 reduce-scatter.1
  269.6 36.0 all-reduce.3

commit v2 on v1

--- a/solution.py
+++ b/solution.py
@@ -1,3 +1,5 @@
+import functools
+
 import jax
 import jax.numpy as jnp
 from jax import lax
@@ -35,7 +37,7 @@
     return lax.broadcasted_iota(jnp.int32, (SPAN, LANES), 1) < feat
 
 
-def state_kernel(x_ref, w_ref, b_ref, fac_ref, s_ref, total_ref, run_ref):
+def state_kernel(x_ref, w_ref, b_ref, fac_ref, prefix_ref, total_ref, run_ref):
     k = pl.program_id(1)
     feat = x_ref.shape[1] // HB
     low = first_lanes(feat)
@@ -51,7 +53,7 @@
         w2 = jnp.where(low, w[:, 2 * j : 2 * j + 1], w[:, 2 * j + 1 : 2 * j + 2])
         weighted = (x_ref[:, sl].astype(F32) * w2).astype(BF16)
         state = dot(weighted, b, 0, 0)
-        s_ref[0, sl, :] = state
+        prefix_ref[0, sl, :] = run_ref[sl, :].astype(BF16)
         for i in range(2):
             rows = slice(i * feat, (i + 1) * feat)
             at = slice(j * LANES + i * feat, j * LANES + (i + 1) * feat)
@@ -60,9 +62,32 @@
     total_ref[...] = run_ref[...].astype(BF16)
 
 
+def entering_of(before_ref, prefix_ref, reach_ref, keep, j, feat):
+    parts = []
+    for i in range(2):
+        h = 2 * j + i
+        at = slice(h * feat, (h + 1) * feat)
+        reach = reach_ref[0, h : h + 1, :]
+        parts.append(
+            before_ref[at, :].astype(F32) * reach + prefix_ref[0, at, :].astype(F32) * keep
+        )
+    return jnp.concatenate(parts, axis=0)
+
+
+def scan_kernel(reverse, part_ref, fac_ref, before_ref):
+    count, own = part_ref.shape[0], fac_ref.shape[1]
+    feat = part_ref.shape[1] // own
+    for h in range(own):
+        at = slice(h * feat, (h + 1) * feat)
+        running = jnp.zeros((feat, part_ref.shape[2]), F32)
+        for d in reversed(range(count)) if reverse else range(count):
+            before_ref[d, at, :] = running.astype(BF16)
+            running = fac_ref[d, h : h + 1, :] * running + part_ref[d, at, :].astype(F32)
+
+
 def out_kernel(
-    x_ref, dy_ref, valid_ref, b_ref, c_ref, ent_ref, col_ref, row_ref, srow_ref, fac_ref,
-    keep_ref, skip_ref,
+    x_ref, dy_ref, valid_ref, b_ref, c_ref, before_ref, prefix_ref, reach_ref, col_ref, row_ref,
+    srow_ref, fac_ref, keep_ref, skip_ref,
     dx_ref, term_ref, total_ref, dcol_ref, dsrow_ref, skip_out_ref, db_ref, dc_ref,
     run_ref, dg_ref,
 ):
@@ -98,7 +123,7 @@
         x2 = x_ref[:, sl]
         dyf = dy_ref[:, sl].astype(F32) * valid
         dy2 = dyf.astype(BF16)
-        e2 = ent_ref[0, sl, :]
+        e2 = entering_of(before_ref, prefix_ref, reach_ref, keep, j, feat).astype(BF16)
         ec2 = jnp.where(low, grown[:, 2 * j : 2 * j + 1], grown[:, 2 * j + 1 : 2 * j + 2])
         dkf = dyf * ec2
         dk2 = dkf.astype(BF16)
@@ -143,7 +168,8 @@
 
 
 def end_kernel(
-    x_ref, w_ref, b_ref, after_ref, term_ref, ent_ref, fac_ref, dx1_ref,
+    x_ref, w_ref, b_ref, after_ref, term_ref, before_ref, prefix_ref, reach_ref, keep_ref, fac_ref,
+    dx1_ref,
     dx_ref, dw_ref, dcot_ref, db_ref,
     carry_ref,
 ):
@@ -153,6 +179,7 @@
     low = first_lanes(feat)
     b = b_ref[...]
     w = w_ref[0, 0]
+    keep = keep_ref[0, 0:1, :]
 
     @pl.when(step == 0)
     def _():
@@ -175,7 +202,7 @@
         dweighted = dot(b, ds_low, 1, 1).astype(BF16).astype(F32)
         dx_ref[:, sl] = (dx1_ref[:, sl].astype(F32) + dweighted * w2).astype(BF16)
         part = dweighted * xf
-        met = ds * ent_ref[0, sl, :].astype(F32)
+        met = ds * entering_of(before_ref, prefix_ref, reach_ref, keep, j, feat)
         for i in range(2):
             h = 2 * j + i
             mine = low if i == 0 else jnp.logical_not(low)
@@ -189,20 +216,24 @@
     db_ref[k] = db_ref[k] + db
 
 
-def scan_heads(total, factor_all, axis, reverse):
+def scan_heads(total, factor_rows, axis, reverse):
     count = lax.axis_size(axis)
     rows, width = total.shape
-    feat = rows // factor_all.shape[1]
     mine = lax.all_to_all(total.reshape(count, rows // count, width), axis, 0, 0)
-    own = factor_all.shape[1] // count
-    here = lax.dynamic_slice_in_dim(factor_all, lax.axis_index(axis) * own, own, axis=1)
-    here = jnp.repeat(here, feat, axis=1)[:, :, None]
-    running = jnp.zeros(mine.shape[1:], F32)
-    before = [None] * count
-    for at in reversed(range(count)) if reverse else range(count):
-        before[at] = running.astype(BF16)
-        running = here[at] * running + mine[at].astype(F32)
-    return lax.all_to_all(jnp.stack(before), axis, 0, 0).reshape(rows, width)
+    before = pl.pallas_call(
+        functools.partial(scan_kernel, reverse),
+        out_shape=jax.ShapeDtypeStruct(mine.shape, BF16),
+        in_specs=[pl.BlockSpec(memory_space=pltpu.VMEM)] * 2,
+        out_specs=pl.BlockSpec(memory_space=pltpu.VMEM),
+        interpret=INTERPRET,
+        name="device_scan",
+    )(mine, factor_rows)
+    return lax.all_to_all(before, axis, 0, 0).reshape(rows, width)
+
+
+def everyones(value, axis):
+    count = lax.axis_size(axis)
+    return lax.all_to_all(jnp.broadcast_to(value[None], (count,) + value.shape), axis, 0, 0)
 
 
 def shards(
@@ -244,7 +275,13 @@
     weights = tail * steps
     decays = jnp.exp(last[:, 0])
     factors = decays * keep[:, None]
-    factor_all = lax.all_gather(jnp.prod(factors, axis=0), "shard")
+    devices = lax.axis_size("shard")
+    factor_here = lax.all_to_all(
+        jnp.prod(factors, axis=0).reshape(devices, heads // devices), "shard", 0, 0
+    )
+    factor_here = jnp.broadcast_to(factor_here[:, :, None], factor_here.shape + (LANES,))
+    reach = jnp.stack([keep[k] * jnp.prod(factors[:k], axis=0) for k in range(spans)])
+    reach_rows = jnp.broadcast_to(reach[:, :, None], (spans, heads, LANES))
 
     def columns(a):
         return a.reshape(spans, SPAN, blocks, HB).transpose(0, 2, 1, 3)
@@ -281,24 +318,18 @@
     row_shape = shape((spans, heads, LANES), F32)
     whole_shape = shape((spans, SPAN, STATE), F32)
 
-    states, total = pl.pallas_call(
+    prefix, total = pl.pallas_call(
         state_kernel,
         grid=(blocks, spans),
         in_specs=[up[n] for n in ("tok", "col", "map", "row")],
         out_specs=[up[n] for n in ("state", "total")],
-        out_shape=[state_shape, total_shape],
+        out_shape=[shape(state_shape.shape, BF16), total_shape],
         scratch_shapes=[pltpu.VMEM((wide, STATE), F32)],
         interpret=INTERPRET,
         name="span_states",
     )(x, w_cols, b_map, fac_rows)
 
-    carry = scan_heads(total, factor_all, "shard", False).astype(F32)
-    entering = []
-    for k in range(spans):
-        entering.append((carry * keep[k]).astype(BF16))
-        if k + 1 < spans:
-            carry = jnp.repeat(factors[k], feat)[:, None] * carry + states[k]
-    entering = jnp.stack(entering)
+    before = scan_heads(total, factor_here, "shard", False)
 
     dx1, terms, back_total, dcols, ds_rows, skip_rows, db1, dc_map = pl.pallas_call(
         out_kernel,
@@ -306,8 +337,8 @@
         in_specs=[
             down[n]
             for n in (
-                "tok", "tok", "valid", "map", "map", "state", "col", "row", "row", "row",
-                "keep", "skip",
+                "tok", "tok", "valid", "map", "map", "total", "state", "row", "col", "row", "row",
+                "row", "keep", "skip",
             )
         ],
         out_specs=[
@@ -331,23 +362,27 @@
         interpret=INTERPRET,
         name="span_out_back",
     )(
-        x, dy, valid[:, :, None], b_map, c_map, entering, c_cols, c_rows, s_rows, fac_rows,
-        keep_rows, skip_lanes,
-    )
-
-    after = scan_heads(back_total, factor_all, "shard", True)
+        x, dy, valid[:, :, None], b_map, c_map, before, prefix, reach_rows, c_cols, c_rows, s_rows,
+        fac_rows, keep_rows, skip_lanes,
+    )
+
+    after = scan_heads(back_total, factor_here, "shard", True)
     dx, dw_cols, dcot_rows, db2 = pl.pallas_call(
         end_kernel,
         grid=(blocks, spans),
         in_specs=[
-            down[n] for n in ("tok", "col", "map", "total", "state", "state", "row", "tok")
+            down[n]
+            for n in (
+                "tok", "col", "map", "total", "state", "total", "state", "row", "keep", "row",
+                "tok",
+            )
         ],
         out_specs=[down[n] for n in ("tok", "col", "row", "whole")],
         out_shape=[shape((tokens, hp), BF16), col_shape, row_shape, whole_shape],
         scratch_shapes=[pltpu.VMEM((wide, STATE), F32)],
         interpret=INTERPRET,
         name="span_end_back",
-    )(x, w_cols, b_map, after, terms, entering, fac_rows, dx1)
+    )(x, w_cols, b_map, after, terms, before, prefix, reach_rows, keep_rows, fac_rows, dx1)
 
     decay_cot = jnp.sum(dcot_rows, axis=2)
     dw = from_columns(dw_cols)
@@ -374,11 +409,13 @@
     back_rows = lax.dot_general(
         joined_cot, gathered, (((1,), (1,)), ((), ())), preferred_element_type=F32
     )
-    summed = lax.psum(shared, "replica").astype(F32)
-    small = lax.psum(
-        jnp.stack([decay_local, jnp.sum(raw_cot, axis=(0, 1)), skip_local]),
-        ("replica", "shard"),
-    )
+    groups = lax.axis_size("replica")
+    pieces = lax.all_to_all(shared.reshape(groups, -1, shared.shape[1]), "replica", 0, 0)
+    piece = jnp.sum(pieces.astype(F32), axis=0).astype(BF16)
+    summed = everyones(piece, "replica").reshape(shared.shape).astype(F32)
+    small = jnp.stack([decay_local, jnp.sum(raw_cot, axis=(0, 1)), skip_local])
+    small = jnp.sum(everyones(small, "shard"), axis=0)
+    small = jnp.sum(everyones(small, "replica"), axis=0)
     return (
         dx[None],
         back_rows.astype(BF16)[None],

time: 317 us -> 299 us (0.943)
  blocking collectives: 58.9 us -> 39.1 us
  other arithmetic: 25.4 us -> 10.1 us
  starting transfers between devices: 14.4 us -> 25.3 us
  Pallas kernels: 62.5 us -> 66.7 us
    psum x1 -> x0, blocking collectives: 39.3 us -> none  [shards(): lax.psum(jnp.stack([decay_local, jnp.sum(raw_cot, axis=(0, 1)), skip_loca...]
    all_to_all x0 -> x2, blocking collectives: none -> 39.1 us  [scan_heads(): lax.all_to_all(total.reshape(count, rows // count, width), axis, 0, 0)]
    reduce_scatter x1, waiting for transfers between devices: 2.82 us -> 37.7 us  [shards(): lax.psum_scatter(grads_local.astype(BF16), 'shard', scatter_dimension=0,...]
    psum x1 -> x0, waiting for transfers between devices: 33.4 us -> none  [shards(): summed = lax.psum(shared, 'replica').astype(F32)]
    unnamed x1 -> x0, blocking collectives: 19.6 us -> none
    unnamed x13 -> x0, other arithmetic: 11.6 us -> none
    all_to_all x4 -> x7, starting transfers between devices: 14.2 us -> 25.2 us  [the longest x3 10 us: everyones(): lax.all_to_all(jnp.broadcast_to(value[None], (count,) + value.shape), axi...]
    pallas_call x0 -> x2, Pallas kernels: none -> 4.82 us  [scan_heads(): pl.pallas_call(functools.partial(scan_kernel, reverse), out_shape=jax.Sha...]
  transfers between devices with their start and end apart: 7 -> 9, of which waited for: 6 -> 7; matrix products, arithmetic and copies ran while one was open for 5% -> 7% of each run, Pallas kernels for 0% -> 4%
where the time goes in v2:
time: 299 us; the launch traced here: 298 us
  waiting for transfers between devices  109 us (36%)
  Pallas kernels  66.7 us (22%)
  blocking collectives  39.1 us (13%)
  starting transfers between devices  25.3 us (8%)
  local copies, waits for them, and re-layouts  22.3 us (7%)
  between operations  14.4 us (5%)
  matrix products  10.7 us (4%)
  other arithmetic  10.1 us (3%)
    all_to_all x2, blocking collectives, scan_heads(): lax.all_to_all(total.reshape(count, rows // count, width), axis, 0, 0)  39.1 us
    reduce_scatter x1, waiting for transfers between devices, shards(): lax.psum_scatter(grads_local.astype(BF16), 'shard', scatter_dimension=0,...  37.7 us
    all_gather x1, waiting for transfers between devices, shards(): gathered = lax.all_gather(joined, 'shard', axis=0, tiled=True)  32 us
    pallas_call x1, Pallas kernels, shards(): pl.pallas_call(out_kernel, grid=(blocks, spans), in_specs=[down[n] for n...  31.7 us
    all_to_all x2, waiting for transfers between devices, scan_heads(): return lax.all_to_all(before, axis, 0, 0).reshape(rows, width)  24.3 us
    pallas_call x1, Pallas kernels, shards(): pl.pallas_call(end_kernel, grid=(blocks, spans), in_specs=[down[n] for n...  17 us
    pallas_call x1, Pallas kernels, shards(): pl.pallas_call(state_kernel, grid=(blocks, spans), in_specs=[up[n] for n...  13.1 us
    all_to_all x3, starting transfers between devices, everyones(): lax.all_to_all(jnp.broadcast_to(value[None], (count,) + value.shape), axi...  10 us
  transfers between devices with their start and end apart: 9, of which 7 were waited for; matrix products, arithmetic and copies ran while one was open for 7% of the time, Pallas kernels for 4%

profile of v2, /device:TPU:0, one launch (start us, length us, event | category | flops | bytes accessed | tf_op | source)
XLA Modules:
  0.0 297.8 jit_solution(18232240089595017491)
XLA Ops:
  7.2 1.1 copy.128
  8.3 1.7 pad_maximum_fusion
  10.1 0.8 reduce-window.4
  13.4 32.0 %all-gather.2.cloned.1.call-done = bf16[4096,320]{1,0:T(8,128)(2,1)} async-done(((bf16[512,320]{1,0:T(8,128)(2,1)}), bf16[4096,320]{1,0:T(8,128)(2,1)}) %all-gather.2.cloned.1.call-update) | async-done | bytes 2621456 | tf_op jit(solution)/shard_map/all_gather | solution.py:263
  45.4 3.2 %fusion.49 = (bf16[256,320]{1,0:T(8,128)(2,1)S(1)}, f32[256,320]{1,0:T(8,128)S(1)}) fusion(bf16[4096,320]{1,0:T(8,128)(2,1)} %all-gather.2.cloned.1.call-done, bf16[1,256,4096]{2,1,0:T(8,128)(2,1)S(1)} %copy-done), kind=kOutput, calls=%fused_computation.81 | convolution fusion | flops 671170560 | bytes 5210112 | tf_op jit(solution)/shard_map/dot_general | solution.py:264
  49.2 0.7 fusion.42
  49.8 1.3 copy.135
  51.9 0.7 all_to_all.31
  52.6 3.3 %all-to-all-start.1 = ((f32[8,1,8]{2,1,0:T(1,128)}), f32[8,1,8]{2,1,0:T(1,128)S(1)}, u32[]{:S(2)}, u32[]{:S(2)}) async-start(f32[8,1,8]{2,1,0:T(1,128)} %bitcast.15), calls=%async_computation.1 | async-start | bytes 8192 | tf_op jit(solution)/shard_map/all_to_all | solution.py:279
  55.9 0.7 broadcast_in_dim.119.fac_ref
  56.6 13.1 %span_states.1 = (bf16[2,4096,128]{2,1,0:T(8,128)(2,1)}, bf16[4096,128]{1,0:T(8,128)(2,1)}) custom-call(bf16[256,4096]{1,0:T(8,128)(2,1)} %bitcast.130, f32[2,8,128,8]{3,2,1,0:T(8,128)} %bitcast.133, bf16[256,128]{1,0:T(8,128)(2,1)} %get-tuple-element.89.b_ref, f32[2,64,128]{2,1,0:T(8,128)} %broadcast_in_dim.119.fac_ref), custom_call_target="tpu_custom_call" | custom-call | tf_op jit(solution)/shard_map/span_states/pallas_call | solution.py:321
  69.7 19.6 %all_to_all.49.part_ref = bf16[8,512,128]{2,1,0:T(8,128)(2,1)} all-to-all(bf16[8,512,128]{2,1,0:T(8,128)(2,1)} %bitcast.146), channel_id=1, replica_groups=mesh['replica'=4,'shard'=8] {'shard'}, dimensions={0} | all-to-all | bytes 2097152 | tf_op jit(solution)/shard_map/all_to_all | solution.py:222
  89.3 0.7 broadcast_in_dim.121.fac_ref
  90.0 2.4 device_scan.2
  92.4 3.6 %all-to-all-start.2 = ((bf16[8,512,128]{2,1,0:T(8,128)(2,1)}), bf16[8,512,128]{2,1,0:T(8,128)(2,1)S(1)}, u32[]{:S(2)}, u32[]{:S(2)}) async-start(bf16[8,512,128]{2,1,0:T(8,128)(2,1)} %device_scan.2), calls=%async_computation.2 | async-start | bytes 2097152 | tf_op jit(solution)/shard_map/all_to_all | solution.py:231
  96.0 0.7 broadcast_in_dim_reshape.3.skip_ref
  97.3 0.7 fusion.9.valid_ref
  98.0 1.3 copy.137
  100.7 10.6 %all-to-all-done.2 = bf16[8,512,128]{2,1,0:T(8,128)(2,1)S(1)} async-done(((bf16[8,512,128]{2,1,0:T(8,128)(2,1)}), bf16[8,512,128]{2,1,0:T(8,128)(2,1)S(1)}, u32[]{:S(2)}, u32[]{:S(2)}) %all-to-all-start.2) | async-done | bytes 1048608 | tf_op jit(solution)/shard_map/all_to_all | solution.py:231
  111.3 0.8 broadcast_in_dim.122.reach_ref
  112.8 31.7 %span_out_back.1 = (bf16[256,4096]{1,0:T(8,128)(2,1)}, f32[2,4096,128]{2,1,0:T(8,128)}, bf16[4096,128]{1,0:T(8,128)(2,1)}, f32[2,8,128,8]{3,2,1,0:T(8,128)}, f32...) custom-call(bf16[256,4096]{1,0:T(8,128)(2,1)} %bitcast.131, ...), custom_call_target="tpu_custom_call" | custom-call | tf_op jit(solution)/shard_map/span_out_back/pallas_call | solution.py:334
  144.5 19.6 %all_to_all.50.part_ref = bf16[8,512,128]{2,1,0:T(8,128)(2,1)} all-to-all(bf16[8,512,128]{2,1,0:T(8,128)(2,1)} %bitcast.145), channel_id=1, replica_groups=mesh['replica'=4,'shard'=8] {'shard'}, dimensions={0} | all-to-all | bytes 2097152 | tf_op jit(solution)/shard_map/all_to_all | solution.py:222
  164.1 2.4 device_scan.3
  166.5 3.7 %all-to-all-start.4 = ((bf16[8,512,128]{2,1,0:T(8,128)(2,1)}), bf16[8,512,128]{2,1,0:T(8,128)(2,1)S(1)}, u32[]{:S(2)}, u32[]{:S(2)}) async-start(bf16[8,512,128]{2,1,0:T(8,128)(2,1)} %device_scan.3), calls=%async_computation.4 | async-start | bytes 2097152 | tf_op jit(solution)/shard_map/all_to_all | solution.py:231
  170.2 1.5 copy.139
  171.8 13.7 %all-to-all-done.4 = bf16[8,512,128]{2,1,0:T(8,128)(2,1)S(1)} async-done(((bf16[8,512,128]{2,1,0:T(8,128)(2,1)}), bf16[8,512,128]{2,1,0:T(8,128)(2,1)S(1)}, u32[]{:S(2)}, u32[]{:S(2)}) %all-to-all-start.4) | async-done | bytes 1048608 | tf_op jit(solution)/shard_map/all_to_all | solution.py:231
  185.5 1.0 copy-done.2
  186.5 17.0 %span_end_back.1 = (bf16[256,4096]{1,0:T(8,128)(2,1)}, f32[2,8,128,8]{3,2,1,0:T(8,128)}, f32[2,64,128]{2,1,0:T(8,128)}, f32[2,128,128]{2,1,0:T(8,128)}) custom-call(bf16[256,4096]{1,0:T(8,128)(2,1)} %bitcast.132, f32[2,8,128,8]{3,2,1,0:T(8,128)} %bitcast.134, bf16[256,128]{1,0:T(8,128)(2,1)} %get-tuple-element.89.b_ref, bf16[4096,128]{1,0:T(8,128)(2,1)} %bitcast.138, ...), custom_call_target="tpu_custom_call" | custom-call | tf_op jit(solution)/shard_map/span_end_back/pallas_call | solution.py:370
  203.5 1.6 copy.138
  205.4 0.9 reduce_sum.98
  207.2 2.4 fusion
  209.6 0.8 copy-done.8
  210.6 0.7 reshape.175
  211.3 3.3 %all-to-all-start.7 = ((f32[8,1,192]{2,1,0:T(1,128)}), f32[8,1,192]{2,1,0:T(1,128)S(1)}, u32[]{:S(2)}, u32[]{:S(2)}) async-start(f32[8,1,192]{2,1,0:T(1,128)} %reshape.175), calls=%async_computation.8 | async-start | bytes 16384 | tf_op jit(solution)/shard_map/all_to_all | solution.py:236
  214.7 37.7 %reduce-scatter.2.cloned.1.call-done = bf16[512,320]{0,1:T(8,128)(2,1)} async-done(((bf16[4096,320]{0,1:T(8,128)(2,1)}), bf16[512,320]{0,1:T(8,128)(2,1)}) %reduce-scatter.2.cloned.1.call-update) | async-done | bytes 327696 | tf_op jit(solution)/shard_map/reduce_scatter | solution.py:408
  252.4 1.8 copy_bitcast_fusion.1
  254.1 4.6 %all-to-all-start.5 = ((bf16[4,128,320]{1,2,0:T(8,128)(2,1)}), bf16[4,128,320]{1,2,0:T(8,128)(2,1)S(1)}, u32[]{:S(2)}, u32[]{:S(2)}) async-start(bf16[4,128,320]{1,2,0:T(8,128)(2,1)} %copy_bitcast_fusion.1), calls=%async_computation.6 | async-start | bytes 655360 | tf_op jit(solution)/shard_map/all_to_all | solution.py:413
  259.2 0.7 reduce.7
  260.0 0.7 reshape.177
  260.7 8.2 %all-to-all-done.5 = bf16[4,128,320]{1,2,0:T(8,128)(2,1)S(1)} async-done(((bf16[4,128,320]{1,2,0:T(8,128)(2,1)}), bf16[4,128,320]{1,2,0:T(8,128)(2,1)S(1)}, u32[]{:S(2)}, u32[]{:S(2)}) %all-to-all-start.5) | async-done | bytes 327712 | tf_op jit(solution)/shard_map/all_to_all | solution.py:413
  268.9 3.2 %all-to-all-start.8 = ((f32[4,1,192]{2,1,0:T(1,128)}), f32[4,1,192]{2,1,0:T(1,128)S(1)}, u32[]{:S(2)}, u32[]{:S(2)}) async-start(f32[4,1,192]{2,1,0:T(1,128)} %reshape.177), calls=%async_computation.9 | async-start | bytes 8192 | tf_op jit(solution)/shard_map/all_to_all | solution.py:236
  272.2 5.5 %all-to-all-done.8 = f32[4,1,192]{2,1,0:T(1,128)S(1)} async-done(((f32[4,1,192]{2,1,0:T(1,128)}), f32[4,1,192]{2,1,0:T(1,128)S(1)}, u32[]{:S(2)}, u32[]{:S(2)}) %all-to-all-start.8) | async-done | bytes 3104 | tf_op jit(solution)/shard_map/all_to_all | solution.py:236
  277.7 0.8 broadcast_in_dim.127
  278.4 3.5 %all-to-all-start.6 = ((bf16[4,128,320]{1,2,0:T(8,128)(2,1)}), bf16[4,128,320]{1,2,0:T(8,128)(2,1)S(1)}, u32[]{:S(2)}, u32[]{:S(2)}) async-start(bf16[4,128,320]{1,2,0:T(8,128)(2,1)} %broadcast_in_dim.127), calls=%async_computation.7 | async-start | bytes 655360 | tf_op jit(solution)/shard_map/all_to_all | solution.py:236
  281.9 4.5 %fusion.1 = bf16[1,256,4096]{2,1,0:T(8,128)(2,1)} fusion(bf16[4096,320]{1,0:T(8,128)(2,1)} %all-gather.2.cloned.1.call-done, bf16[256,64]{1,0:T(8,128)(2,1)S(1)} %bitcast.152, bf16[256,128]{1,0:T(8,128)(2,1)S(1)} %bitcast.148, bf16[256,128]{1,0:T(8,128)(2,1)S(1)} %bitcast.150), kind=kOutput, calls=%fused_computation.3 | convolution fusion | flops 672628736 | bytes 4882432 | tf_op jit(solution)/shard_map/dot_general | solution.py:409
  286.4 0.7 reduce.8
  287.7 1.5 all-to-all-done.6
  289.9 1.0 copy.149
  (76 shorter events, 9.9 us)
Async XLA Ops:
  7.2 38.2 %copy-start = (bf16[1,256,4096]{2,1,0:T(8,128)(2,1)S(1)}, bf16[1,256,4096]{2,1,0:T(8,128)(2,1)}, u32[]{:S(2)}) copy-start(bf16[1,256,4096]{2,1,0:T(8,128)(2,1)} %param.10) | copy-start | bytes 6291460
  7.2 38.2 %all-gather.2.cloned.1.call-start = ((), (), s32[]{:S(2)}) async-start(), calls=%async_computation.10 | async-start | bytes 3538944 | tf_op jit(solution)/shard_map/all_gather | solution.py:263
  13.4 35.2 %copy-start.9 = (f32[64]{0:T(128)S(1)}, f32[64]{0:T(128)}, u32[]{:S(2)}) copy-start(f32[64]{0:T(128)} %param.18) | copy-start | bytes 772
  49.0 49.1 %copy-start.3 = (f32[2,64,128]{2,1,0:T(8,128)}, f32[2,64,128]{2,1,0:T(8,128)S(1)}, u32[]{:S(2)}) copy-start(f32[2,64,128]{2,1,0:T(8,128)S(1)} %fusion.18.row_ref) | copy-start | bytes 196612
  52.6 17.2 %all-to-all-start.1 = ((f32[8,1,8]{2,1,0:T(1,128)}), f32[8,1,8]{2,1,0:T(1,128)S(1)}, u32[]{:S(2)}, u32[]{:S(2)}) async-start(f32[8,1,8]{2,1,0:T(1,128)} %bitcast.15), calls=%async_computation.1 | async-start | bytes 8192 | tf_op jit(solution)/shard_map/all_to_all | solution.py:279
  90.0 6.0 %copy-start.10 = (f32[64]{0:T(128)S(1)}, f32[64]{0:T(128)}, u32[]{:S(2)}) copy-start(f32[64]{0:T(128)} %param.19) | copy-start | bytes 772
  92.4 18.9 %all-to-all-start.2 = ((bf16[8,512,128]{2,1,0:T(8,128)(2,1)}), bf16[8,512,128]{2,1,0:T(8,128)(2,1)S(1)}, u32[]{:S(2)}, u32[]{:S(2)}) async-start(bf16[8,512,128]{2,1,0:T(8,128)(2,1)} %device_scan.2), calls=%async_computation.2 | async-start | bytes 2097152 | tf_op jit(solution)/shard_map/all_to_all | solution.py:231
  111.3 1.5 copy-start.1
  166.5 5.3 %copy-start.5 = (f32[2,128,128]{2,1,0:T(8,128)S(1)}, f32[2,128,128]{2,1,0:T(8,128)}, u32[]{:S(2)}) copy-start(f32[2,128,128]{2,1,0:T(8,128)} %get-tuple-element.29) | copy-start | bytes 393220
  166.5 19.0 %all-to-all-start.4 = ((bf16[8,512,128]{2,1,0:T(8,128)(2,1)}), bf16[8,512,128]{2,1,0:T(8,128)(2,1)S(1)}, u32[]{:S(2)}, u32[]{:S(2)}) async-start(bf16[8,512,128]{2,1,0:T(8,128)(2,1)} %device_scan.3), calls=%async_computation.4 | async-start | bytes 2097152 | tf_op jit(solution)/shard_map/all_to_all | solution.py:231
  170.2 82.2 %reduce-scatter.2.cloned.1.call-start = ((), (), s32[]{:S(2)}) async-start(), calls=%async_computation.11 | async-start | bytes 2949120 | tf_op jit(solution)/shard_map/reduce_scatter | solution.py:408
  185.5 1.0 copy-start.2
  186.4 18.6 %copy-start.4 = (f32[2,64,128]{2,1,0:T(8,128)S(1)}, f32[2,64,128]{2,1,0:T(8,128)}, u32[]{:S(2)}) copy-start(f32[2,64,128]{2,1,0:T(8,128)} %copy-done.3) | copy-start | bytes 196612
  186.5 20.1 %copy-start.11 = (f32[2,64,128]{2,1,0:T(8,128)S(1)}, f32[2,64,128]{2,1,0:T(8,128)}, u32[]{:S(2)}) copy-start(f32[2,64,128]{2,1,0:T(8,128)} %get-tuple-element.30) | copy-start | bytes 196612
  203.5 3.7 %copy-start.6 = (f32[2,128,128]{2,1,0:T(8,128)S(1)}, f32[2,128,128]{2,1,0:T(8,128)}, u32[]{:S(2)}) copy-start(f32[2,128,128]{2,1,0:T(8,128)} %get-tuple-element.27) | copy-start | bytes 393220
  203.5 3.7 %copy-start.7 = (f32[2,128,128]{2,1,0:T(8,128)S(1)}, f32[2,128,128]{2,1,0:T(8,128)}, u32[]{:S(2)}) copy-start(f32[2,128,128]{2,1,0:T(8,128)} %get-tuple-element.28) | copy-start | bytes 393220
  209.5 0.8 copy-start.8
  209.5 1.0 copy-start.12
  211.3 42.8 %all-to-all-start.7 = ((f32[8,1,192]{2,1,0:T(1,128)}), f32[8,1,192]{2,1,0:T(1,128)S(1)}, u32[]{:S(2)}, u32[]{:S(2)}) async-start(f32[8,1,192]{2,1,0:T(1,128)} %reshape.175), calls=%async_computation.8 | async-start | bytes 16384 | tf_op jit(solution)/shard_map/all_to_all | solution.py:236
  254.1 14.8 %all-to-all-start.5 = ((bf16[4,128,320]{1,2,0:T(8,128)(2,1)}), bf16[4,128,320]{1,2,0:T(8,128)(2,1)S(1)}, u32[]{:S(2)}, u32[]{:S(2)}) async-start(bf16[4,128,320]{1,2,0:T(8,128)(2,1)} %copy_bitcast_fusion.1), calls=%async_computation.6 | async-start | bytes 655360 | tf_op jit(solution)/shard_map/all_to_all | solution.py:413
  268.9 8.8 %all-to-all-start.8 = ((f32[4,1,192]{2,1,0:T(1,128)}), f32[4,1,192]{2,1,0:T(1,128)S(1)}, u32[]{:S(2)}, u32[]{:S(2)}) async-start(f32[4,1,192]{2,1,0:T(1,128)} %reshape.177), calls=%async_computation.9 | async-start | bytes 8192 | tf_op jit(solution)/shard_map/all_to_all | solution.py:236
  278.4 10.7 %all-to-all-start.6 = ((bf16[4,128,320]{1,2,0:T(8,128)(2,1)}), bf16[4,128,320]{1,2,0:T(8,128)(2,1)S(1)}, u32[]{:S(2)}, u32[]{:S(2)}) async-start(bf16[4,128,320]{1,2,0:T(8,128)(2,1)} %broadcast_in_dim.127), calls=%async_computation.7 | async-start | bytes 655360 | tf_op jit(solution)/shard_map/all_to_all | solution.py:236
Sparse Core Ops, SparseCore 0:
  10.4 34.8 all-gather.1
  209.7 42.6 reduce-scatter.1

commit v3 on v2

--- a/solution.py
+++ b/solution.py
@@ -367,6 +367,10 @@
     )
 
     after = scan_heads(back_total, factor_here, "shard", True)
+    dc_low = dc_map.astype(BF16).reshape(tokens, STATE)
+    c_grads = dot(token_rows, dc_low, 0, 0).astype(BF16)
+    c_grads, after = lax.optimization_barrier((c_grads, after))
+    c_shared = lax.psum_scatter(c_grads, "shard", scatter_dimension=0, tiled=True)
     dx, dw_cols, dcot_rows, db2 = pl.pallas_call(
         end_kernel,
         grid=(blocks, spans),
@@ -398,27 +402,26 @@
         skip_rows[:, :, : HB // 2].reshape(spans, heads, feat), axis=(0, 2)
     )
     db = (db1 + db2).astype(BF16).reshape(tokens, STATE)
-    joined_cot = jnp.concatenate(
-        [db, dc_map.astype(BF16).reshape(tokens, STATE), raw_cot.astype(BF16).reshape(tokens, -1)],
-        axis=1,
-    )
-    grads_local = lax.dot_general(
-        token_rows, joined_cot, (((0,), (0,)), ((), ())), preferred_element_type=F32
-    )
-    shared = lax.psum_scatter(grads_local.astype(BF16), "shard", scatter_dimension=0, tiled=True)
-    back_rows = lax.dot_general(
-        joined_cot, gathered, (((1,), (1,)), ((), ())), preferred_element_type=F32
-    )
+    raw_low = raw_cot.astype(BF16).reshape(tokens, -1)
+    joined_cot = jnp.concatenate([db, dc_low, raw_low], axis=1)
+    grads = dot(token_rows, jnp.concatenate([db, raw_low], axis=1), 0, 0).astype(BF16)
+    grads, c_shared = lax.optimization_barrier((grads, c_shared))
+    shared = lax.psum_scatter(grads, "shard", scatter_dimension=0, tiled=True)
+    back_rows = dot(joined_cot, gathered, 1, 1).astype(BF16)
+    small = jnp.stack([decay_local, jnp.sum(raw_cot, axis=(0, 1)), skip_local])
+    small = jnp.sum(everyones(small, "shard"), axis=0)
+    small = jnp.sum(everyones(small, "replica"), axis=0)
+    shared, c_shared, back_rows, small = lax.optimization_barrier(
+        (shared, c_shared, back_rows, small)
+    )
+    shared = jnp.concatenate([shared[:, :STATE], c_shared, shared[:, STATE:]], axis=1)
     groups = lax.axis_size("replica")
     pieces = lax.all_to_all(shared.reshape(groups, -1, shared.shape[1]), "replica", 0, 0)
     piece = jnp.sum(pieces.astype(F32), axis=0).astype(BF16)
     summed = everyones(piece, "replica").reshape(shared.shape).astype(F32)
-    small = jnp.stack([decay_local, jnp.sum(raw_cot, axis=(0, 1)), skip_local])
-    small = jnp.sum(everyones(small, "shard"), axis=0)
-    small = jnp.sum(everyones(small, "replica"), axis=0)
     return (
         dx[None],
-        back_rows.astype(BF16)[None],
+        back_rows[None],
         summed[:, : 2 * STATE],
         summed[:, 2 * STATE :],
         small[0],

time: 299 us -> 302 us (1.010)
  blocking collectives: 39.1 us -> 60.9 us
  waiting for transfers between devices: 109 us -> 97.6 us
  starting transfers between devices: 25.3 us -> 18.6 us
    all_to_all x0 -> x2, blocking collectives: none -> 21.7 us  [the longest x1 14.5 us: shards(): lax.all_to_all(shared.reshape(groups, -1, shared.shape[1]), 'replica', 0, 0)]
    all_to_all x1 -> x0, waiting for transfers between devices: 8.17 us -> none  [shards(): lax.all_to_all(shared.reshape(groups, -1, shared.shape[1]), 'replica', 0, 0)]
    reduce_scatter x1 -> x2, waiting for transfers between devices: 37.7 us -> 31.8 us  [the longest x1 21.1 us: shards(): shared = lax.psum_scatter(grads, 'shard', scatter_dimension=0, tiled=True)]
    all_to_all x1 -> x0, starting transfers between devices: 4.61 us -> none  [shards(): lax.all_to_all(shared.reshape(groups, -1, shared.shape[1]), 'replica', 0, 0)]
    all_to_all x3 -> x2, waiting for transfers between devices: 6.96 us -> 9.33 us  [everyones(): lax.all_to_all(jnp.broadcast_to(value[None], (count,) + value.shape), axi...]
    all_to_all x3 -> x2, starting transfers between devices: 10 us -> 8.05 us  [everyones(): lax.all_to_all(jnp.broadcast_to(value[None], (count,) + value.shape), axi...]
    dot_general x2 -> x3, matrix products: 6.88 us -> 7.81 us  [dot(): lax.dot_general(a, b, (((ca,), (cb,)), ((), ())), preferred_element_type=...]
  transfers between devices with their start and end apart: 9 -> 8, of which waited for: 7 -> 7; matrix products, arithmetic and copies ran while one was open for 7% -> 9% of each run, Pallas kernels for 4% -> 10%
where the time goes in v3:
time: 302 us; the launch traced here: 300 us
  waiting for transfers between devices  97.6 us (32%)
  Pallas kernels  66.9 us (22%)
  blocking collectives  60.9 us (20%)
  local copies, waits for them, and re-layouts  20.2 us (7%)
  starting transfers between devices  18.6 us (6%)
  between operations  14.1 us (5%)
  matrix products  11.7 us (4%)
  other arithmetic  10.2 us (3%)
    all_to_all x2, blocking collectives, scan_heads(): lax.all_to_all(total.reshape(count, rows // count, width), axis, 0, 0)  39.1 us
    all_gather x1, waiting for transfers between devices, shards(): gathered = lax.all_gather(joined, 'shard', axis=0, tiled=True)  32 us
    pallas_call x1, Pallas kernels, shards(): pl.pallas_call(out_kernel, grid=(blocks, spans), in_specs=[down[n] for n...  31.7 us
    all_to_all x2, waiting for transfers between devices, scan_heads(): return lax.all_to_all(before, axis, 0, 0).reshape(rows, width)  24.4 us
    reduce_scatter x1, waiting for transfers between devices, shards(): shared = lax.psum_scatter(grads, 'shard', scatter_dimension=0, tiled=True)  21.1 us
    pallas_call x1, Pallas kernels, shards(): pl.pallas_call(end_kernel, grid=(blocks, spans), in_specs=[down[n] for n...  17.2 us
    all_to_all x1, blocking collectives, shards(): lax.all_to_all(shared.reshape(groups, -1, shared.shape[1]), 'replica', 0, 0)  14.5 us
    pallas_call x1, Pallas kernels, shards(): pl.pallas_call(state_kernel, grid=(blocks, spans), in_specs=[up[n] for n...  13.1 us
  transfers between devices with their start and end apart: 8, of which 7 were waited for; matrix products, arithmetic and copies ran while one was open for 9% of the time, Pallas kernels for 10%

profile of v3, /device:TPU:0, one launch (start us, length us, event | category | flops | bytes accessed | tf_op | source)
XLA Modules:
  0.0 300.1 jit_solution(15213509076539018213)
XLA Ops:
  7.2 1.1 copy.133
  8.3 1.7 pad_maximum_fusion
  10.1 0.8 reduce-window.4
  13.4 32.0 %all-gather.2.cloned.1.call-done = bf16[4096,320]{1,0:T(8,128)(2,1)} async-done(((bf16[512,320]{1,0:T(8,128)(2,1)}), bf16[4096,320]{1,0:T(8,128)(2,1)}) %all-gather.2.cloned.1.call-update) | async-done | bytes 2621456 | tf_op jit(solution)/shard_map/all_gather | solution.py:263
  45.4 3.2 %fusion.58 = (bf16[256,320]{1,0:T(8,128)(2,1)S(1)}, f32[256,320]{1,0:T(8,128)S(1)}) fusion(bf16[4096,320]{1,0:T(8,128)(2,1)} %all-gather.2.cloned.1.call-done, bf16[1,256,4096]{2,1,0:T(8,128)(2,1)S(1)} %copy-done), kind=kOutput, calls=%fused_computation.91 | convolution fusion | flops 671170560 | bytes 5210112 | tf_op jit(solution)/shard_map/dot_general | solution.py:264
  49.8 0.7 fusion.51
  50.6 0.7 all_to_all.31
  51.3 3.3 %all-to-all-start.1 = ((f32[8,1,8]{2,1,0:T(1,128)}), f32[8,1,8]{2,1,0:T(1,128)S(1)}, u32[]{:S(2)}, u32[]{:S(2)}) async-start(f32[8,1,8]{2,1,0:T(1,128)} %bitcast.15), calls=%async_computation.1 | async-start | bytes 8192 | tf_op jit(solution)/shard_map/all_to_all | solution.py:279
  54.6 1.3 copy.140
  55.9 0.7 broadcast_in_dim.119.fac_ref
  56.6 13.1 %span_states.1 = (bf16[2,4096,128]{2,1,0:T(8,128)(2,1)}, bf16[4096,128]{1,0:T(8,128)(2,1)}) custom-call(bf16[256,4096]{1,0:T(8,128)(2,1)} %bitcast.134, f32[2,8,128,8]{3,2,1,0:T(8,128)} %bitcast.137, bf16[256,128]{1,0:T(8,128)(2,1)} %get-tuple-element.105.b_ref, f32[2,64,128]{2,1,0:T(8,128)} %broadcast_in_dim.119.fac_ref), custom_call_target="tpu_custom_call" | custom-call | tf_op jit(solution)/shard_map/span_states/pallas_call | solution.py:321
  69.7 19.6 %all_to_all.49.part_ref = bf16[8,512,128]{2,1,0:T(8,128)(2,1)} all-to-all(bf16[8,512,128]{2,1,0:T(8,128)(2,1)} %bitcast.151), channel_id=1, replica_groups=mesh['replica'=4,'shard'=8] {'shard'}, dimensions={0} | all-to-all | bytes 2097152 | tf_op jit(solution)/shard_map/all_to_all | solution.py:222
  89.3 0.7 broadcast_in_dim.121.fac_ref
  90.0 2.4 device_scan.2
  92.4 3.6 %all-to-all-start.2 = ((bf16[8,512,128]{2,1,0:T(8,128)(2,1)}), bf16[8,512,128]{2,1,0:T(8,128)(2,1)S(1)}, u32[]{:S(2)}, u32[]{:S(2)}) async-start(bf16[8,512,128]{2,1,0:T(8,128)(2,1)} %device_scan.2), calls=%async_computation.2 | async-start | bytes 2097152 | tf_op jit(solution)/shard_map/all_to_all | solution.py:231
  96.0 0.7 broadcast_in_dim_reshape.3.skip_ref
  97.3 0.7 fusion.18.valid_ref
  98.1 1.3 copy.142
  100.7 10.6 %all-to-all-done.2 = bf16[8,512,128]{2,1,0:T(8,128)(2,1)S(1)} async-done(((bf16[8,512,128]{2,1,0:T(8,128)(2,1)}), bf16[8,512,128]{2,1,0:T(8,128)(2,1)S(1)}, u32[]{:S(2)}, u32[]{:S(2)}) %all-to-all-start.2) | async-done | bytes 1048608 | tf_op jit(solution)/shard_map/all_to_all | solution.py:231
  111.3 0.8 broadcast_in_dim.123.keep_ref
  112.0 0.7 broadcast_in_dim.122.reach_ref
  112.8 31.7 %span_out_back.1 = (bf16[256,4096]{1,0:T(8,128)(2,1)}, f32[2,4096,128]{2,1,0:T(8,128)}, bf16[4096,128]{1,0:T(8,128)(2,1)}, f32[2,8,128,8]{3,2,1,0:T(8,128)}, f32...) custom-call(bf16[256,4096]{1,0:T(8,128)(2,1)} %bitcast.135, ...), custom_call_target="tpu_custom_call" | custom-call | tf_op jit(solution)/shard_map/span_out_back/pallas_call | solution.py:334
  144.5 19.6 %all_to_all.50.part_ref = bf16[8,512,128]{2,1,0:T(8,128)(2,1)} all-to-all(bf16[8,512,128]{2,1,0:T(8,128)(2,1)} %bitcast.150), channel_id=1, replica_groups=mesh['replica'=4,'shard'=8] {'shard'}, dimensions={0} | all-to-all | bytes 2097152 | tf_op jit(solution)/shard_map/all_to_all | solution.py:222
  164.1 2.4 device_scan.3
  166.5 3.6 %all-to-all-start.4 = ((bf16[8,512,128]{2,1,0:T(8,128)(2,1)}), bf16[8,512,128]{2,1,0:T(8,128)(2,1)S(1)}, u32[]{:S(2)}, u32[]{:S(2)}) async-start(bf16[8,512,128]{2,1,0:T(8,128)(2,1)} %device_scan.3), calls=%async_computation.4 | async-start | bytes 2097152 | tf_op jit(solution)/shard_map/all_to_all | solution.py:231
  170.1 1.4 fusion.1
  171.6 13.8 %all-to-all-done.4 = bf16[8,512,128]{2,1,0:T(8,128)(2,1)S(1)} async-done(((bf16[8,512,128]{2,1,0:T(8,128)(2,1)}), bf16[8,512,128]{2,1,0:T(8,128)(2,1)S(1)}, u32[]{:S(2)}, u32[]{:S(2)}) %all-to-all-start.4) | async-done | bytes 1048608 | tf_op jit(solution)/shard_map/all_to_all | solution.py:231
  185.5 1.8 copy.144
  187.3 17.2 %span_end_back.1 = (bf16[256,4096]{1,0:T(8,128)(2,1)}, f32[2,8,128,8]{3,2,1,0:T(8,128)}, f32[2,64,128]{2,1,0:T(8,128)}, f32[2,128,128]{2,1,0:T(8,128)}) custom-call(bf16[256,4096]{1,0:T(8,128)(2,1)} %bitcast.136, f32[2,8,128,8]{3,2,1,0:T(8,128)} %bitcast.138, bf16[256,128]{1,0:T(8,128)(2,1)} %get-tuple-element.105.b_ref, bf16[4096,128]{1,0:T(8,128)(2,1)} %bitcast.141, ...), custom_call_target="tpu_custom_call" | custom-call | tf_op jit(solution)/shard_map/span_end_back/pallas_call | solution.py:374
  204.5 1.0 reduce_sum.98
  205.6 1.5 copy.143
  208.2 1.8 fusion
  210.0 10.7 %reduce-scatter.3.cloned.1.call-done = bf16[512,128]{0,1:T(8,128)(2,1)} async-done(((bf16[4096,128]{0,1:T(8,128)(2,1)}), bf16[512,128]{0,1:T(8,128)(2,1)}) %reduce-scatter.3.cloned.1.call-update) | async-done | bytes 131088 | tf_op jit(solution)/shard_map/reduce_scatter | solution.py:373
  221.1 7.3 %all_to_all.51 = f32[8,1,192]{2,1,0:T(1,128)S(1)} all-to-all(f32[8,1,192]{2,1,0:T(1,128)S(1)} %reshape.175), channel_id=1, replica_groups=mesh['replica'=4,'shard'=8] {'shard'}, dimensions={0} | all-to-all | bytes 12288 | tf_op jit(solution)/shard_map/all_to_all | solution.py:236
  228.8 0.7 reduce.7
  229.6 0.7 reshape.177
  230.3 4.6 %all-to-all-start.6 = ((f32[4,1,192]{2,1,0:T(1,128)}), f32[4,1,192]{2,1,0:T(1,128)S(1)}, u32[]{:S(2)}, u32[]{:S(2)}) async-start(f32[4,1,192]{2,1,0:T(1,128)} %reshape.177), calls=%async_computation.8 | async-start | bytes 8192 | tf_op jit(solution)/shard_map/all_to_all | solution.py:236
  234.9 4.6 %convolution_convert_fusion = bf16[256,4096]{1,0:T(8,128)(2,1)} fusion(bf16[4096,320]{1,0:T(8,128)(2,1)} %all-gather.2.cloned.1.call-done, bf16[256,64]{1,0:T(8,128)(2,1)S(1)} %bitcast.155, bf16[256,128]{1,0:T(8,128)(2,1)S(1)} %bitcast.157, bf16[256,128]{1,0:T(8,128)(2,1)S(1)} %bitcast.153), kind=kOutput, calls=%fused_computation | convolution fusion | flops 672628736 | bytes 4882432 | tf_op jit(solution)/shard_map/dot_general | solution.py:33
  239.5 1.0 all-to-all-done.6
  241.2 21.1 %reduce-scatter.5.cloned.1.call-done = bf16[512,192]{0,1:T(8,128)(2,1)} async-done(((bf16[4096,192]{0,1:T(8,128)(2,1)}), bf16[512,192]{0,1:T(8,128)(2,1)}) %reduce-scatter.5.cloned.1.call-update) | async-done | bytes 196624 | tf_op jit(solution)/shard_map/reduce_scatter | solution.py:409
  262.3 0.8 slice.56
  263.2 0.9 slice.55
  264.2 14.5 %all_to_all.52 = bf16[4,128,320]{1,2,0:T(8,128)(2,1)S(1)} all-to-all(bf16[4,128,320]{1,2,0:T(8,128)(2,1)S(1)} %copy_bitcast_fusion.1), channel_id=1, replica_groups=mesh['replica'=4,'shard'=8] {'replica'}, dimensions={0} | all-to-all | bytes 655360 | tf_op jit(solution)/shard_map/all_to_all | solution.py:419
  278.7 0.8 broadcast_in_dim.129
  279.5 3.5 %all-to-all-start.8 = ((bf16[4,128,320]{1,2,0:T(8,128)(2,1)}), bf16[4,128,320]{1,2,0:T(8,128)(2,1)S(1)}, u32[]{:S(2)}, u32[]{:S(2)}) async-start(bf16[4,128,320]{1,2,0:T(8,128)(2,1)} %broadcast_in_dim.129), calls=%async_computation.10 | async-start | bytes 655360 | tf_op jit(solution)/shard_map/all_to_all | solution.py:236
  283.4 8.3 %all-to-all-done.8 = bf16[4,128,320]{1,2,0:T(8,128)(2,1)S(1)} async-done(((bf16[4,128,320]{1,2,0:T(8,128)(2,1)}), bf16[4,128,320]{1,2,0:T(8,128)(2,1)S(1)}, u32[]{:S(2)}, u32[]{:S(2)}) %all-to-all-start.8) | async-done | bytes 327712 | tf_op jit(solution)/shard_map/all_to_all | solution.py:236
  291.9 0.7 slice.67
  292.6 1.0 copy.155
  (82 shorter events, 9.5 us)
Async XLA Ops:
  7.2 38.2 %copy-start = (bf16[1,256,4096]{2,1,0:T(8,128)(2,1)S(1)}, bf16[1,256,4096]{2,1,0:T(8,128)(2,1)}, u32[]{:S(2)}) copy-start(bf16[1,256,4096]{2,1,0:T(8,128)(2,1)} %param.10) | copy-start | bytes 6291460
  7.2 38.2 %all-gather.2.cloned.1.call-start = ((), (), s32[]{:S(2)}) async-start(), calls=%async_computation.11 | async-start | bytes 3538944 | tf_op jit(solution)/shard_map/all_gather | solution.py:263
  13.4 35.9 %copy-start.10 = (f32[64]{0:T(128)S(1)}, f32[64]{0:T(128)}, u32[]{:S(2)}) copy-start(f32[64]{0:T(128)} %param.18) | copy-start | bytes 772
  49.6 48.4 %copy-start.3 = (f32[2,64,128]{2,1,0:T(8,128)}, f32[2,64,128]{2,1,0:T(8,128)S(1)}, u32[]{:S(2)}) copy-start(f32[2,64,128]{2,1,0:T(8,128)S(1)} %fusion.27.row_ref) | copy-start | bytes 196612
  51.3 18.5 %all-to-all-start.1 = ((f32[8,1,8]{2,1,0:T(1,128)}), f32[8,1,8]{2,1,0:T(1,128)S(1)}, u32[]{:S(2)}, u32[]{:S(2)}) async-start(f32[8,1,8]{2,1,0:T(1,128)} %bitcast.15), calls=%async_computation.1 | async-start | bytes 8192 | tf_op jit(solution)/shard_map/all_to_all | solution.py:279
  90.0 6.0 %copy-start.11 = (f32[64]{0:T(128)S(1)}, f32[64]{0:T(128)}, u32[]{:S(2)}) copy-start(f32[64]{0:T(128)} %param.19) | copy-start | bytes 772
  92.4 18.9 %all-to-all-start.2 = ((bf16[8,512,128]{2,1,0:T(8,128)(2,1)}), bf16[8,512,128]{2,1,0:T(8,128)(2,1)S(1)}, u32[]{:S(2)}, u32[]{:S(2)}) async-start(bf16[8,512,128]{2,1,0:T(8,128)(2,1)} %device_scan.2), calls=%async_computation.2 | async-start | bytes 2097152 | tf_op jit(solution)/shard_map/all_to_all | solution.py:231
  111.3 1.5 copy-start.1
  164.1 6.1 %copy-start.6 = (f32[2,128,128]{2,1,0:T(8,128)S(1)}, f32[2,128,128]{2,1,0:T(8,128)}, u32[]{:S(2)}) copy-start(f32[2,128,128]{2,1,0:T(8,128)} %get-tuple-element.31) | copy-start | bytes 393220
  166.5 18.9 %all-to-all-start.4 = ((bf16[8,512,128]{2,1,0:T(8,128)(2,1)}), bf16[8,512,128]{2,1,0:T(8,128)(2,1)S(1)}, u32[]{:S(2)}, u32[]{:S(2)}) async-start(bf16[8,512,128]{2,1,0:T(8,128)(2,1)} %device_scan.3), calls=%async_computation.4 | async-start | bytes 2097152 | tf_op jit(solution)/shard_map/all_to_all | solution.py:231
  170.1 50.6 %reduce-scatter.3.cloned.1.call-start = ((), (), s32[]{:S(2)}) async-start(), calls=%async_computation.12 | async-start | bytes 1179648 | tf_op jit(solution)/shard_map/reduce_scatter | solution.py:373
  185.4 1.9 copy-start.2
  185.4 76.9 %reduce-scatter.5.cloned.1.call-start = ((), (), s32[]{:S(2)}) async-start(), calls=%async_computation.13 | async-start | bytes 1769472 | tf_op jit(solution)/shard_map/reduce_scatter | solution.py:409
  187.3 19.9 %copy-start.4 = (f32[2,64,128]{2,1,0:T(8,128)S(1)}, f32[2,64,128]{2,1,0:T(8,128)}, u32[]{:S(2)}) copy-start(f32[2,64,128]{2,1,0:T(8,128)} %copy-done.3) | copy-start | bytes 196612
  187.3 20.3 %copy-start.12 = (f32[2,64,128]{2,1,0:T(8,128)S(1)}, f32[2,64,128]{2,1,0:T(8,128)}, u32[]{:S(2)}) copy-start(f32[2,64,128]{2,1,0:T(8,128)} %get-tuple-element.39) | copy-start | bytes 196612
  204.5 3.7 %copy-start.7 = (f32[2,128,128]{2,1,0:T(8,128)S(1)}, f32[2,128,128]{2,1,0:T(8,128)}, u32[]{:S(2)}) copy-start(f32[2,128,128]{2,1,0:T(8,128)} %get-tuple-element.37) | copy-start | bytes 393220
  204.5 3.7 %copy-start.8 = (f32[2,128,128]{2,1,0:T(8,128)S(1)}, f32[2,128,128]{2,1,0:T(8,128)}, u32[]{:S(2)}) copy-start(f32[2,128,128]{2,1,0:T(8,128)} %get-tuple-element.38) | copy-start | bytes 393220
  208.2 12.5 %copy-start.9 = (f32[2,8,8,128]{3,2,1,0:T(8,128)S(1)}, f32[2,8,8,128]{3,2,1,0:T(8,128)}, u32[]{:S(2)}) copy-start(f32[2,8,8,128]{3,2,1,0:T(8,128)} %get-tuple-element.46) | copy-start | bytes 196612
  208.2 12.7 %copy-start.13 = (f32[64]{0:T(128)S(1)}, f32[64]{0:T(128)}, u32[]{:S(2)}) copy-start(f32[64]{0:T(128)} %param.17) | copy-start | bytes 772
  230.3 10.2 %all-to-all-start.6 = ((f32[4,1,192]{2,1,0:T(1,128)}), f32[4,1,192]{2,1,0:T(1,128)S(1)}, u32[]{:S(2)}, u32[]{:S(2)}) async-start(f32[4,1,192]{2,1,0:T(1,128)} %reshape.177), calls=%async_computation.8 | async-start | bytes 8192 | tf_op jit(solution)/shard_map/all_to_all | solution.py:236
  234.9 29.2 %copy-start.5 = (bf16[512,128]{0,1:T(8,128)(2,1)S(1)}, bf16[512,128]{0,1:T(8,128)(2,1)}, u32[]{:S(2)}) copy-start(bf16[512,128]{0,1:T(8,128)(2,1)} %reduce-scatter.3.cloned.1.call-done) | copy-start | bytes 393220
  279.5 12.3 %all-to-all-start.8 = ((bf16[4,128,320]{1,2,0:T(8,128)(2,1)}), bf16[4,128,320]{1,2,0:T(8,128)(2,1)S(1)}, u32[]{:S(2)}, u32[]{:S(2)}) async-start(bf16[4,128,320]{1,2,0:T(8,128)(2,1)} %broadcast_in_dim.129), calls=%async_computation.10 | async-start | bytes 655360 | tf_op jit(solution)/shard_map/all_to_all | solution.py:236
Sparse Core Ops, SparseCore 0:
  10.4 34.8 all-gather.1
  185.5 35.1 reduce-scatter.2
  224.0 38.2 reduce-scatter.4
